TPU v7x, 32 devices: a whole 2x2x4 slice. The times are simulated.
32 devices in a mesh: ens: 2 (over x), lon: 16 (over z, y, core).
Axes of the slice: x: 2, y: 2, z: 4, core: 2. Of those that a mesh axis runs over, the one named last changes fastest.
Arguments:
- tracer: float32 [4, 256, 75, 256], P(None, 'lon', None, 'ens'), parts along dimension 3, may hold values from -6 to 6
- east_speed: float32 [256, 75, 256], P('lon', None, 'ens'), parts along dimension 2, may hold values from -0.25 to 0.25
- north_speed: float32 [256, 75, 256], P('lon', None, 'ens'), parts along dimension 2, may hold values from -0.25 to 0.25
- diffusivity: float32 [256, 75, 256], P('lon', None, 'ens'), parts along dimension 2, may hold values from 0.02 to 0.2
- mixing: float32 [256, 75, 256], P('lon', None, 'ens'), parts along dimension 2, may hold values from 0.05 to 5
- thickness: float32 [256, 75, 256], P('lon', None, 'ens'), parts along dimension 2, may hold values from 0.5 to 2
- depth_levels: int32 [256, 256], P('lon', 'ens'), parts along dimension 1, may hold values from 0 to 75
- air_flux: float32 [8, 4096], P('ens', 'lon'), parts along dimension 0, may hold values from -6 to 6
- margin_tile: int32 [32768, 1], P(('ens', 'lon')), parts along dimension 0, may hold values from 0 to 15; in each aligned block of 1024 rows (0 to 1023, 1024 to 2047, ...) at most 64 rows name the same one
- margin_source: int32 [32768], P(('ens', 'lon')), parts along dimension 0, may hold values from 0 to 255
- margin_cell: int32 [32768], P(('ens', 'lon')), parts along dimension 0, may hold values from 0 to 2047
- margin_weight: float32 [32768], P(('ens', 'lon')), parts along dimension 0, may hold values from 0.2 to 1
Outputs:
- tracer_next: float32 [4, 256, 75, 256], P(None, 'lon', None, 'ens'), parts along dimension 3
There are 2 independent parts, one for each index of `ens`. A program takes and returns all parts, laid end to end along the dimension named above; each array names one. Nothing has to cross between parts.
Inputs may be any that keep to these rules, and one draw needn't show every extreme that they name: `margin_tile`: the rows of one tile name each ocean tile at most 64 times.
All inputs are finite; a program needn't handle non-finite values.
Results may differ from a plain program's by a relative error of at most 0.00002.
Values sent between devices are 32-bit elements; how exact they have to be, the bound alone decides.
A program may use at most 192 MiB of HBM per device.

v0:
```python
import jax
import jax.numpy as jnp
from jax import lax
from jax.sharding import PartitionSpec as P

CAP = 64


def padded_2(shard, sides, width):
    for axis, dim in sides:
        size, length = (lax.axis_size(axis), shard.shape[dim])
        up = [(i, (i + 1) % size) for i in range(size)]
        down = [(j, i) for i, j in up]
        last = lax.slice_in_dim(shard, length - width, length, axis=dim)
        leading = lax.slice_in_dim(shard, 0, width, axis=dim)
        before = lax.ppermute(last, axis, up)
        after = lax.ppermute(leading, axis, down)
        shard = jnp.concatenate([before, shard, after], axis=dim)
    return shard


def from_partner(block, axis, apart):
    count = lax.axis_size(axis)
    route = []
    for low in range(count):
        high = low | 1 << apart
        if high != low and high < count:
            route += [(low, high), (high, low)]
    return lax.ppermute(block, axis, route)


def face_flux(speed, kappa_near, kappa_far, open_face, near, far):
    return open_face * (
        jnp.maximum(speed, 0.0) * near
        + jnp.minimum(speed, 0.0) * far
        + 0.5 * (kappa_near + kappa_far) * (near - far)
    )


def mix_columns(stepped, mixing, thickness, wet_mask, surface):
    levels = stepped.shape[2]
    wet_below = jnp.concatenate([wet_mask[:, 1:], jnp.zeros_like(wet_mask[:, :1])], axis=1)
    thickness_below = jnp.concatenate([thickness[:, 1:], thickness[:, -1:]], axis=1)
    coupling = mixing * wet_below / (0.5 * (thickness + thickness_below))
    prior_coupling = jnp.zeros_like(thickness[:, 0])
    prior_gain = jnp.zeros_like(thickness[:, 0])
    prior_value = jnp.zeros_like(stepped[:, :, 0])
    gain_list = []
    value_list = []
    for level_index in range(levels):
        here_coupling = coupling[:, level_index]
        here_thickness = thickness[:, level_index]
        pivot_value = here_thickness + here_coupling + prior_coupling - prior_coupling * prior_gain
        right_side = here_thickness * stepped[:, :, level_index]
        if level_index == 0:
            right_side = right_side + wet_mask[:, 0] * surface
        prior_value = (right_side + prior_coupling * prior_value) / pivot_value
        prior_gain = here_coupling / pivot_value
        prior_coupling = here_coupling
        gain_list.append(prior_gain)
        value_list.append(prior_value)
    solved = [value_list[-1]]
    for level_index in range(levels - 2, -1, -1):
        solved.append(value_list[level_index] + gain_list[level_index] * solved[-1])
    return jnp.stack(solved[::-1], axis=2)


def shards(
    tracer,
    east_speed,
    north_speed,
    diffusivity,
    mixing,
    thickness,
    depth_levels,
    air_flux,
    margin_tile,
    margin_source,
    margin_cell,
    margin_weight,
):
    lon_cells, levels, lat_cells = east_speed.shape
    tracer_count = tracer.shape[0]
    cycle_size = lax.axis_size("lon")
    level_ids = jnp.arange(levels, dtype=jnp.int32)
    wet_mask = (level_ids[None, :, None] < depth_levels[:, None, :]).astype(jnp.float32)
    stacked = jnp.concatenate([tracer, east_speed[None], diffusivity[None], wet_mask[None]], axis=0)
    edges = jnp.concatenate([stacked[:, :1], stacked[:, -1:]], axis=1)
    edge_halo = padded_2(edges, (("lon", 1),), 1)
    padded = jnp.concatenate([edge_halo[:, :1], stacked, edge_halo[:, 3:]], axis=1)
    padded_speed = padded[tracer_count]
    padded_kappa = padded[tracer_count + 1]
    padded_wet = padded[tracer_count + 2]
    east_flux = face_flux(
        padded_speed[None, :-1],
        padded_kappa[None, :-1],
        padded_kappa[None, 1:],
        (padded_wet[:-1] * padded_wet[1:])[None],
        padded[:tracer_count, :-1],
        padded[:tracer_count, 1:],
    )
    zonal_change = east_flux[:, 1:] - east_flux[:, :-1]
    top_rows = jnp.concatenate(
        [
            tracer[:, :, :, -1],
            north_speed[None, :, :, -1],
            diffusivity[None, :, :, -1],
            wet_mask[None, :, :, -1],
        ],
        axis=0,
    )
    mirror = top_rows
    for bit_index in range(cycle_size.bit_length() - 1):
        mirror = from_partner(mirror, "lon", bit_index)
    mirror = jnp.flip(mirror, axis=1)
    fold_flux = face_flux(
        (0.5 * (north_speed[:, :, -1] - mirror[tracer_count]))[None],
        diffusivity[None, :, :, -1],
        mirror[tracer_count + 1][None],
        (wet_mask[:, :, -1] * mirror[tracer_count + 2])[None],
        tracer[:, :, :, -1],
        mirror[:tracer_count],
    )
    inner_flux = face_flux(
        north_speed[None, :, :, :-1],
        diffusivity[None, :, :, :-1],
        diffusivity[None, :, :, 1:],
        (wet_mask[:, :, :-1] * wet_mask[:, :, 1:])[None],
        tracer[:, :, :, :-1],
        tracer[:, :, :, 1:],
    )
    north_flux = jnp.concatenate([inner_flux, fold_flux[..., None]], axis=3)
    south_flux = jnp.concatenate([jnp.zeros_like(inner_flux[..., :1]), inner_flux], axis=3)
    stepped = tracer - zonal_change - (north_flux - south_flux)
    dest_tile = margin_tile[:, 0]
    payload = margin_weight[None, :] * jnp.take(air_flux, margin_source, axis=1)
    onehot = (dest_tile[:, None] == jnp.arange(cycle_size, dtype=jnp.int32)[None, :]).astype(
        jnp.int32
    )
    before = jnp.cumsum(onehot, axis=0) - onehot
    slot_index = jnp.sum(before * onehot, axis=1)
    position = dest_tile * CAP + slot_index
    values = jnp.zeros((tracer_count, cycle_size * CAP), jnp.float32).at[:, position].set(payload)
    cell_ids = jnp.zeros((1, cycle_size * CAP), jnp.int32).at[0, position].set(margin_cell)
    received, received_cells = (
        lax.all_to_all(values, "lon", split_axis=1, concat_axis=1, tiled=True),
        lax.all_to_all(cell_ids, "lon", split_axis=1, concat_axis=1, tiled=True),
    )
    surface = (
        jnp.zeros((tracer_count, lon_cells * lat_cells), jnp.float32)
        .at[:, received_cells[0]]
        .add(received)
    )
    surface = surface.reshape(tracer_count, lon_cells, lat_cells)
    return mix_columns(stepped, mixing, thickness, wet_mask, surface)


def solution(mesh):
    placed = (
        P(None, "lon", None, "ens"),
        P("lon", None, "ens"),
        P("lon", None, "ens"),
        P("lon", None, "ens"),
        P("lon", None, "ens"),
        P("lon", None, "ens"),
        P("lon", "ens"),
        P("ens", "lon"),
        P(("ens", "lon"), None),
        P(("ens", "lon")),
        P(("ens", "lon")),
        P(("ens", "lon")),
    )
    return jax.shard_map(
        shards, mesh=mesh, in_specs=placed, out_specs=P(None, "lon", None, "ens"), check_vma=False
    )
```

profile of v0, /device:TPU:0, one launch (start us, length us, event | category | flops | bytes accessed | tf_op | source)
XLA Modules:
  0.0 142.0 jit_solution(13267512229541679027)
XLA Ops:
  0.8 3.4 %pad_maximum_fusion.5 = (f32[7,1,75,128]{3,1,0,2:T(1,128)}, f32[7,1,75,128]{3,1,0,2:T(1,128)}) fusion(f32[1,16,75,128]{3,1,0,2:T(8,128)S(1)} %fusion.7, f32[1,16,75,128]{3,1,0,2:T(8,128)} %bitcast.2261, f32[1,16,75,128]{3,1,0,2:T(8,128)} %bitcast.2265, f32[4,16,75,128]{3,1,2,0:T(8,128)} %param.12), kind=kLoop, calls=%fused_computation.39 | loop fusion | flops 403200 | bytes 4838400 | tf_op jit(solution)/shard_map/slice | solution.py:88
  4.6 5.0 %collective-permute-start.1 = (f32[7,1,75,128]{3,1,0,2:T(1,128)}, f32[7,1,75,128]{3,1,0,2:T(1,128)}, u32[]{:S(2)}, u32[]{:S(2)}) collective-permute-start(f32[7,1,75,128]{3,1,0,2:T(1,128)} %get-tuple-element.198), channel_id=1, source_target_pairs={{1,0},{2,1},{3,2},{4,3},{5,4},{6,5},{7,6},{8,7},{9,8},{10,9},{11,1... | collective-permute-start | bytes 806408 | tf_op jit(solution)/shard_map/ppermute | solution.py:17
  9.7 2.1 %slice.825 = f32[4,16,75,1]{3,1,2,0:T(8,128)} slice(f32[4,16,75,128]{3,1,2,0:T(8,128)S(1)} %copy-done), slice={[0:4], [0:16], [0:75], [127:128]} | slice | bytes 38400 | tf_op jit(solution)/shard_map/slice | solution.py:105
  15.3 2.7 %copy.27985 = f32[4,16,75,1]{2,1,0,3:T(8,128)S(1)} copy(f32[4,16,75,1]{3,1,2,0:T(8,128)} %slice.825) | data formatting | bytes 38400 | tf_op jit(solution)/shard_map/slice | solution.py:105
  19.4 2.1 %slice.826 = f32[16,75,1]{2,0,1:T(8,128)} slice(f32[16,75,128]{2,0,1:T(8,128)} %param.14), slice={[0:16], [0:75], [127:128]} | slice | bytes 9600 | tf_op jit(solution)/shard_map/slice | solution.py:106
  23.6 4.5 %reduce-window.6 = s32[16,8,128]{2,1,0:T(8,128)S(1)} reduce-window(s32[16,8,128]{2,1,0:T(8,128)S(1)} %fusion.21, s32[]{:T(128)} %constant.11.clone.1), window={size=1x1x128 pad=0_0x0_0x127_0}, to_apply=%region_0.1 | reduce-window | flops 2080768 | bytes 131076 | tf_op jit(solution)/shard_map/reduce-window
  28.8 4.5 %scatter_custom_fusion.2 = s32[1024]{0:T(1024)S(1)} fusion(s32[1024]{0:T(1024)S(1)} %broadcast_select_fusion, s32[1024]{0:T(1024)} %param.22, s32[]{:T(128)} %constant.11.clone.1), kind=kCustom, calls=%fused_computation.739 | custom fusion | bytes 4608
  33.9 4.2 %all-to-all-start = ((s32[1,16,64]{2,0,1:T(1,128)}), s32[1,16,64]{2,0,1:T(1,128)}, u32[]{:S(2)}, u32[]{:S(2)}) async-start(s32[1,16,64]{2,0,1:T(1,128)} %bitcast.23), calls=%async_computation | async-start | bytes 16384 | tf_op jit(solution)/shard_map/all_to_all | solution.py:147
  53.7 2.7 %add_multiply_fusion.1 = f32[4,16,75,127]{3,1,0,2:T(8,128)} fusion(f32[16,75,127]{2,0,1:T(8,128)S(1)} %get-tuple-element.405, f32[16,75,127]{2,0,1:T(8,128)S(1)} %get-tuple-element.395, f32[16,75,127]{2,0,1:T(8,128)S(1)} %get-tuple-element.394, f32[16,75,127]{2,0,1:T(8,128)S(1)} %get-tuple-element.404, f32[4,16,75,128]{3,1,2,0:T(8,128)S(1)} %copy-done), kind=kLoop, calls=%fused_computation.11 | loop fusion | flops 4267200 | bytes 9811200 | tf_op jit(solution)/shard_map/mul | solution.py:33
  62.6 2.4 %collective-permute-done.3 = f32[7,16,75]{2,1,0:T(8,128)} collective-permute-done((f32[7,16,75]{2,1,0:T(8,128)}, f32[7,16,75]{2,1,0:T(8,128)}, u32[]{:S(2)}, u32[]{:S(2)}) %collective-permute-start.3) | collective-permute-done | bytes 33632 | tf_op jit(solution)/shard_map/ppermute | solution.py:29
  68.0 7.6 %scatter_custom_fusion = f32[4,1024]{0,1:T(8,128)} fusion(s32[1024]{0:T(1024)} %bitcast.2282, f32[1024]{0:T(1024)} %param.23, f32[]{:T(128)} %constant.17.clone.1, f32[]{:T(128)} %constant.9.clone.1, pred[1024]{0:T(1024)(128)(4,1)} %compare_and_fusion, f32[4,256]{0,1:T(8,128)S(1)} %copy.27992, s32[1024]{0:T(1024)} %fusion.221), kind=kCustom, calls=%fused_computation.31 | custom fusion | flops 8192 | bytes 30720 | tf_op jit(solution)/shard_map/scatter | solution.py:143
  77.6 4.7 %all-to-all-start.1 = ((f32[16,1,256]{2,1,0:T(1,128)}), f32[16,1,256]{2,1,0:T(1,128)S(1)}, u32[]{:S(2)}, u32[]{:S(2)}) async-start(f32[16,1,256]{2,1,0:T(1,128)} %reshape.23109), calls=%async_computation.1 | async-start | bytes 32768 | tf_op jit(solution)/shard_map/all_to_all | solution.py:146
  84.2 2.8 %collective-permute-start.5 = (f32[7,16,75]{2,1,0:T(8,128)}, f32[7,16,75]{2,1,0:T(8,128)}, u32[]{:S(2)}, u32[]{:S(2)}) collective-permute-start(f32[7,16,75]{2,1,0:T(8,128)} %collective-permute-done.4), channel_id=1, source_target_pairs={{0,8},{8,0},{1,9},{9,1},{2,10},{10,2},{3,11},{11,3},{4,12},{12,4},... | collective-permute-start | bytes 100808 | tf_op jit(solution)/shard_map/ppermute | solution.py:29
  87.1 1.7 %all-to-all-done.1 = f32[16,1,256]{2,1,0:T(1,128)S(1)} async-done(((f32[16,1,256]{2,1,0:T(1,128)}), f32[16,1,256]{2,1,0:T(1,128)S(1)}, u32[]{:S(2)}, u32[]{:S(2)}) %all-to-all-start.1) | async-done | bytes 16416 | tf_op jit(solution)/shard_map/all_to_all | solution.py:146
  91.1 7.4 %scatter_custom_fusion.1 = f32[4,2048]{0,1:T(8,128)} fusion(s32[1024]{0:T(1024)S(1)} %bitcast.2285, f32[1024,4]{1,0:T(8,128)} %bitcast.2272, f32[]{:T(128)} %constant.9.clone.1), kind=kCustom, calls=%fused_computation.34 | custom fusion | flops 4096 | bytes 33280 | tf_op jit(solution)/shard_map/scatter-add | solution.py:152
  105.2 3.3 %copy.27988 = f32[4,16,75,1]{3,1,0,2:T(8,128)} copy(f32[4,16,75,1]{2,1,0,3:T(8,128)S(1)} %multiply_bitcast_fusion) | data formatting | bytes 38400 | tf_op jit(solution)/shard_map/broadcast_in_dim | solution.py:132
  108.6 2.8 %maximum_bitcast_fusion = (f32[17,75,128]{2,0,1:T(8,128)S(1)}, f32[1,17,75,128]{3,1,0,2:T(8,128)S(1)}, f32[17,75,128]{2,0,1:T(8,128)}) fusion(f32[1,16,75,128]{3,1,0,2:T(8,128)} %copy-done.4, f32[1,16,75,128]{3,1,0,2:T(8,128)S(1)} %bitcast.2262, f32[1,16,75,128]{3,1,0,2:T(8,128)} %bitcast.2266, f32[7,1,75,128]{3,1,0,2:T(1,128)S(1)} %collective-permute-done, ...), kind=kLoop, calls=%fused_computation.19 | loop fusion | flops 2284800 | bytes 6796800 | tf_op jit(solution)/shard_map/mul | solution.py:34
  111.4 3.3 %maximum_maximum_fusion = (f32[7,17,75,128]{3,1,0,2:T(8,128)S(1)}, f32[7,17,75,128]{3,1,0,2:T(8,128)S(1)}) fusion(f32[1,16,75,128]{3,1,0,2:T(8,128)S(1)} %copy-done.5, f32[1,16,75,128]{3,1,0,2:T(8,128)S(1)} %bitcast.2263, f32[1,16,75,128]{3,1,0,2:T(8,128)S(1)} %bitcast.2267, f32[7,1,75,128]{3,1,0,2:T(1,128)S(1)} %collective-permute-done, ...), kind=kLoop, calls=%fused_computation.4 | loop fusion | flops 9139200 | bytes 13977600 | tf_op jit(solution)/shard_map/concatenate | solution.py:90
  114.7 2.2 %fusion.3 = (f32[17,75,128]{2,0,1:T(8,128)}, f32[17,75,128]{2,0,1:T(8,128)}) fusion(f32[7,1,75,128]{3,1,0,2:T(1,128)} %collective-permute-done.1, f32[1,16,75,128]{3,1,0,2:T(8,128)S(1)} %copy-done.5, f32[1,16,75,128]{3,1,0,2:T(8,128)S(1)} %bitcast.2264, f32[1,16,75,128]{3,1,0,2:T(8,128)S(1)} %bitcast.2268, f32[7,1,75,128]{3,1,0,2:T(1,128)S(1)} %collective-permute-done, ...), kind=kLoop, calls=%fused_computation.14 | loop fusion | flops 1795200 | bytes 6796800 | tf_op jit(solution)/shard_map/mul | solution.py:36
  116.9 3.5 %add_multiply_fusion = f32[4,17,75,128]{3,1,0,2:T(8,128)S(1)} fusion(f32[7,17,75,128]{3,1,0,2:T(8,128)S(1)} %get-tuple-element.196, f32[7,17,75,128]{3,1,0,2:T(8,128)S(1)} %get-tuple-element.195, f32[17,75,128]{2,0,1:T(8,128)} %get-tuple-element.401, f32[17,75,128]{2,0,1:T(8,128)} %get-tuple-element.402, f32[17,75,128]{2,0,1:T(8,128)S(1)} %get-tuple-element.192, ...), kind=kLoop, calls=%fused_computation.6 | loop fusion | flops 4569600 | bytes 10444800 | tf_op jit(solution)/shard_map/mul | solution.py:33
  120.9 3.2 %fusion.1 = f32[4,16,75,128]{3,1,0,2:T(8,128)S(1)} fusion(f32[4,17,75,128]{3,1,0,2:T(8,128)S(1)} %add_multiply_fusion, f32[4,16,75,1]{3,1,0,2:T(8,128)} %copy.27988, f32[4,16,75,127]{3,1,0,2:T(8,128)S(1)} %copy-done.7, f32[4,16,75,128]{3,1,2,0:T(8,128)S(1)} %copy-done), kind=kLoop, calls=%fused_computation.9 | loop fusion | flops 3072000 | bytes 12288000 | tf_op jit(solution)/shard_map/sub | solution.py:134
  125.7 3.0 %fusion.41 = (f32[4,16,128]{2,1,0:T(8,128)S(1)}, f32[4,16,128]{2,1,0:T(8,128)S(1)}, f32[4,16,128]{2,1,0:T(8,128)S(1)}, f32[4,16,128]{2,1,0:T(8,128)S(1)}, f32[4,...) fusion(f32[4,16,75,128]{3,1,0,2:T(8,128)S(1)} %fusion.1, ...), kind=kLoop, calls=%fused_computation.156 | loop fusion | flops 2162688 | bytes 4669440 | tf_op jit(solution)/shard_map/div | solution.py:57
  129.1 2.8 %constant_dynamic-update-slice_fusion.74 = (f32[4,16,75,128]{3,1,0,2:T(8,128)S(1)}, f32[4,16,128]{2,1,0:T(8,128)S(1)}, f32[4,16,128]{2,1,0:T(8,128)S(1)}, f32[4,...) fusion(f32[16,128]{1,0:T(8,128)} %get-tuple-element.191, ...), kind=kLoop, calls=%fused_computation.118 | loop fusion | flops 2818047 | bytes 5185536
  135.8 3.5 %constant_dynamic-update-slice_fusion.62 = (f32[4,16,75,128]{3,1,0,2:T(8,128)S(1)}, f32[4,16,1,128]{3,1,0,2:T(8,128)S(1)}, f32[4,16,1,128]{3,1,0,2:T(8,128)S(1)}...) fusion(f32[4,16,75,128]{3,1,0,2:T(8,128)S(1)} %constant_dynamic, ...), kind=kLoop, calls=%fused_computation.106 | loop fusion | flops 3014656 | bytes 5021696
  (467 shorter events, 53.6 us)
Async XLA Ops:
  4.2 104.4 %collective-permute-start = (f32[7,1,75,128]{3,1,0,2:T(1,128)}, f32[7,1,75,128]{3,1,0,2:T(1,128)S(1)}, u32[]{:S(2)}, u32[]{:S(2)}) collective-permute-start(f32[7,1,75,128]{3,1,0,2:T(1,128)} %get-tuple-element.197), channel_id=1, source_target_pairs={{0,1},{1,2},{2,3},{3,4},{4,5},{5,6},{6,7},{7,8},{8,9},{9,10},{10,1... | collective-permute-start | bytes 806408 | tf_op jit(solution)/shard_map/ppermute | solution.py:16
  4.6 103.9 %collective-permute-start.1 = (f32[7,1,75,128]{3,1,0,2:T(1,128)}, f32[7,1,75,128]{3,1,0,2:T(1,128)}, u32[]{:S(2)}, u32[]{:S(2)}) collective-permute-start(f32[7,1,75,128]{3,1,0,2:T(1,128)} %get-tuple-element.198), channel_id=1, source_target_pairs={{1,0},{2,1},{3,2},{4,3},{5,4},{6,5},{7,6},{8,7},{9,8},{10,9},{11,1... | collective-permute-start | bytes 806408 | tf_op jit(solution)/shard_map/ppermute | solution.py:17
  15.3 13.3 %copy-start.153 = (s32[2]{0:T(128)S(1)}, s32[2]{0:T(128)}, u32[]{:S(2)}) copy-start(s32[2]{0:T(128)} %constant.53) | copy-start | bytes 28
  23.5 36.9 %collective-permute-start.2 = (f32[7,16,75]{2,1,0:T(8,128)}, f32[7,16,75]{2,1,0:T(8,128)}, u32[]{:S(2)}, u32[]{:S(2)}) collective-permute-start(f32[7,16,75]{2,1,0:T(8,128)} %pad_maximum_fusion.6), channel_id=1, source_target_pairs={{0,1},{1,0},{2,3},{3,2},{4,5},{5,4},{6,7},{7,6},{8,9},{9,8},{10,11... | collective-permute-start | bytes 100808 | tf_op jit(solution)/shard_map/ppermute | solution.py:29
  33.9 43.7 %all-to-all-start = ((s32[1,16,64]{2,0,1:T(1,128)}), s32[1,16,64]{2,0,1:T(1,128)}, u32[]{:S(2)}, u32[]{:S(2)}) async-start(s32[1,16,64]{2,0,1:T(1,128)} %bitcast.23), calls=%async_computation | async-start | bytes 16384 | tf_op jit(solution)/shard_map/all_to_all | solution.py:147
  42.7 13.7 %copy-start.34 = (f32[16,128]{1,0:T(8,128)}, f32[16,128]{1,0:T(8,128)S(1)}, u32[]{:S(2)}) copy-start(f32[16,128]{1,0:T(8,128)S(1)} %get-tuple-element.153) | copy-start | bytes 24580
  42.7 13.7 %copy-start.131 = (f32[16,128]{1,0:T(8,128)}, f32[16,128]{1,0:T(8,128)S(1)}, u32[]{:S(2)}) copy-start(f32[16,128]{1,0:T(8,128)S(1)} %get-tuple-element.181) | copy-start | bytes 24580
  42.8 13.7 %copy-start.132 = (f32[16,128]{1,0:T(8,128)}, f32[16,128]{1,0:T(8,128)S(1)}, u32[]{:S(2)}) copy-start(f32[16,128]{1,0:T(8,128)S(1)} %get-tuple-element.183) | copy-start | bytes 24580
  42.8 13.7 %copy-start.133 = (f32[16,128]{1,0:T(8,128)}, f32[16,128]{1,0:T(8,128)S(1)}, u32[]{:S(2)}) copy-start(f32[16,128]{1,0:T(8,128)S(1)} %get-tuple-element.185) | copy-start | bytes 24580
  42.8 13.7 %copy-start.134 = (f32[16,128]{1,0:T(8,128)}, f32[16,128]{1,0:T(8,128)S(1)}, u32[]{:S(2)}) copy-start(f32[16,128]{1,0:T(8,128)S(1)} %get-tuple-element.187) | copy-start | bytes 24580
  42.8 13.7 %copy-start.135 = (f32[16,128]{1,0:T(8,128)}, f32[16,128]{1,0:T(8,128)S(1)}, u32[]{:S(2)}) copy-start(f32[16,128]{1,0:T(8,128)S(1)} %get-tuple-element.189) | copy-start | bytes 24580
  42.8 13.7 %copy-start.136 = (f32[16,128]{1,0:T(8,128)}, f32[16,128]{1,0:T(8,128)S(1)}, u32[]{:S(2)}) copy-start(f32[16,128]{1,0:T(8,128)S(1)} %get-tuple-element.180) | copy-start | bytes 24580
  42.8 13.7 %copy-start.137 = (f32[16,128]{1,0:T(8,128)}, f32[16,128]{1,0:T(8,128)S(1)}, u32[]{:S(2)}) copy-start(f32[16,128]{1,0:T(8,128)S(1)} %get-tuple-element.182) | copy-start | bytes 24580
  42.8 13.7 %copy-start.138 = (f32[16,128]{1,0:T(8,128)}, f32[16,128]{1,0:T(8,128)S(1)}, u32[]{:S(2)}) copy-start(f32[16,128]{1,0:T(8,128)S(1)} %get-tuple-element.184) | copy-start | bytes 24580
  42.8 13.7 %copy-start.139 = (f32[16,128]{1,0:T(8,128)}, f32[16,128]{1,0:T(8,128)S(1)}, u32[]{:S(2)}) copy-start(f32[16,128]{1,0:T(8,128)S(1)} %get-tuple-element.186) | copy-start | bytes 24580
  42.8 13.7 %copy-start.140 = (f32[16,128]{1,0:T(8,128)}, f32[16,128]{1,0:T(8,128)S(1)}, u32[]{:S(2)}) copy-start(f32[16,128]{1,0:T(8,128)S(1)} %get-tuple-element.188) | copy-start | bytes 24580
  42.8 13.7 %copy-start.141 = (f32[16,128]{1,0:T(8,128)}, f32[16,128]{1,0:T(8,128)S(1)}, u32[]{:S(2)}) copy-start(f32[16,128]{1,0:T(8,128)S(1)} %get-tuple-element.190) | copy-start | bytes 24580
  60.5 4.6 %collective-permute-start.3 = (f32[7,16,75]{2,1,0:T(8,128)}, f32[7,16,75]{2,1,0:T(8,128)}, u32[]{:S(2)}, u32[]{:S(2)}) collective-permute-start(f32[7,16,75]{2,1,0:T(8,128)} %collective-permute-done.2), channel_id=1, source_target_pairs={{0,2},{2,0},{1,3},{3,1},{4,6},{6,4},{5,7},{7,5},{8,10},{10,8},{9,1... | collective-permute-start | bytes 100808 | tf_op jit(solution)/shard_map/ppermute | solution.py:29
  65.1 19.2 %collective-permute-start.4 = (f32[7,16,75]{2,1,0:T(8,128)}, f32[7,16,75]{2,1,0:T(8,128)}, u32[]{:S(2)}, u32[]{:S(2)}) collective-permute-start(f32[7,16,75]{2,1,0:T(8,128)} %collective-permute-done.3), channel_id=1, source_target_pairs={{0,4},{4,0},{1,5},{5,1},{2,6},{6,2},{3,7},{7,3},{8,12},{12,8},{9,1... | collective-permute-start | bytes 100808 | tf_op jit(solution)/shard_map/ppermute | solution.py:29
  75.6 26.9 %copy-start.145 = (f32[16,75,1]{1,0,2:T(8,128)S(1)}, f32[16,75,1]{1,0,2:T(8,128)}, u32[]{:S(2)}) copy-start(f32[16,75,1]{1,0,2:T(8,128)} %copy-done.144) | copy-start | bytes 14404
  75.6 26.9 %copy-start.147 = (f32[16,75,1]{1,0,2:T(8,128)S(1)}, f32[16,75,1]{1,0,2:T(8,128)}, u32[]{:S(2)}) copy-start(f32[16,75,1]{1,0,2:T(8,128)} %copy-done.146) | copy-start | bytes 14404
  75.6 27.5 %copy-start.143 = (f32[16,75,1]{1,0,2:T(8,128)S(1)}, f32[16,75,1]{1,0,2:T(8,128)}, u32[]{:S(2)}) copy-start(f32[16,75,1]{1,0,2:T(8,128)} %copy-done.142) | copy-start | bytes 14404
  77.6 11.2 %all-to-all-start.1 = ((f32[16,1,256]{2,1,0:T(1,128)}), f32[16,1,256]{2,1,0:T(1,128)S(1)}, u32[]{:S(2)}, u32[]{:S(2)}) async-start(f32[16,1,256]{2,1,0:T(1,128)} %reshape.23109), calls=%async_computation.1 | async-start | bytes 32768 | tf_op jit(solution)/shard_map/all_to_all | solution.py:146
  84.2 17.4 %collective-permute-start.5 = (f32[7,16,75]{2,1,0:T(8,128)}, f32[7,16,75]{2,1,0:T(8,128)}, u32[]{:S(2)}, u32[]{:S(2)}) collective-permute-start(f32[7,16,75]{2,1,0:T(8,128)} %collective-permute-done.4), channel_id=1, source_target_pairs={{0,8},{8,0},{1,9},{9,1},{2,10},{10,2},{3,11},{11,3},{4,12},{12,4},... | collective-permute-start | bytes 100808 | tf_op jit(solution)/shard_map/ppermute | solution.py:29
  (140 other events, 754.3 us)
where the time goes:
time: 144 us; the launch traced here: 142 us
  other arithmetic  72.8 us (51%)
  local copies, waits for them, and re-layouts  42 us (29%)
  starting transfers between devices  20.3 us (14%)
  waiting for transfers between devices  4.13 us (3%)
  between operations  2.83 us (2%)
    unnamed x40, other arithmetic  10.3 us
    sub x13, other arithmetic, mix_columns(): here_thickness + here_coupling + prior_coupling  9.39 us
    unnamed x349, local copies, waits for them, and re-layouts  7.9 us
    scatter x1, other arithmetic, shards(): jnp.zeros((tracer_count, cycle_size * CAP), jnp.float32).at[:, position]  7.59 us
    scatter-add x1, other arithmetic, shards(): surface = jnp.zeros((tracer_count, lon_cells * lat_cells), jnp.float32).a...  7.4 us
    mul x3, other arithmetic, face_flux(): open_face * (jnp.maximum(speed, 0.0) * near + jnp.minimum(speed, 0.0) * f...  6.84 us
    ppermute x4, starting transfers between devices, from_partner(): return lax.ppermute(block, axis, route)  5.91 us
    ppermute x1, starting transfers between devices, padded_2(): after = lax.ppermute(leading, axis, down)  4.99 us
  transfers between devices with their start and end apart: 8, of which 2 were waited for; matrix products, arithmetic and copies ran while one was open for 54% of the time, Pallas kernels for 0%

commit v1 on v0

v1 whole, which is shorter than its diff:
```python
import jax
import jax.numpy as jnp
from jax import lax
from jax.experimental import pallas as pl
from jax.experimental.pallas import tpu as pltpu
from jax.sharding import PartitionSpec as P

CAP = 64
LANES = 128
ROWS = 16
F32 = jnp.float32
BF16 = jnp.bfloat16
I32 = jnp.int32


def iota(shape, axis):
    return lax.broadcasted_iota(I32, shape, axis)


def thirds(x):
    high = x.astype(BF16).astype(F32)
    rest = x - high
    middle = rest.astype(BF16).astype(F32)
    return high, middle, rest - middle


def prepare(tiles, tile_ref, source_ref, cell_ref, weight_ref, air_ref, tracer_ref, north_ref,
            kappa_ref, top_ref, send_ref):
    count, lon_cells = tracer_ref.shape[:2]
    records = tile_ref.shape[1]
    air_cells = air_ref.shape[1]
    lane = iota((tracer_ref.shape[2], LANES), 1)

    def take(i, packed):
        columns = [tracer_ref[n, i] for n in range(count)] + [north_ref[i], kappa_ref[i]]
        for f, column in enumerate(columns):
            spot = f * lon_cells + i
            packed = jnp.where(lane == spot, pltpu.roll(column, spot + 1, 1), packed)
        return packed

    top_ref[...] = lax.fori_loop(0, lon_cells, take, jnp.zeros(top_ref.shape, F32))

    picks = (iota((air_cells, records), 0) == source_ref[...]).astype(F32).astype(BF16)
    parts = jnp.concatenate(thirds(air_ref[...]), axis=0).astype(BF16)
    found = jnp.dot(parts, picks, preferred_element_type=F32)
    found = found[:count] + (found[count:2 * count] + found[2 * count:])
    payload = weight_ref[...] * found

    chosen = (iota((tiles, records), 0) == tile_ref[...]).astype(F32)
    earlier = (iota((LANES, LANES), 0) < iota((LANES, LANES), 1)).astype(F32).astype(BF16)
    carried = jnp.zeros((tiles, 1), F32)
    slots = []
    for start in range(0, records, LANES):
        piece = chosen[:, start:start + LANES]
        rank = jnp.dot(piece.astype(BF16), earlier, preferred_element_type=F32) + carried
        slots.append(jnp.sum(piece * rank, axis=0, keepdims=True))
        carried = carried + jnp.sum(piece, axis=1, keepdims=True)
    slot = jnp.concatenate(slots, axis=1)
    places = (iota((CAP, records), 0).astype(F32) == slot).astype(F32).astype(BF16)

    cells = cell_ref[...]
    row = (cells // LANES).astype(F32)
    column = (cells % LANES).astype(F32)
    lines = [p[n:n + 1] for p in thirds(payload) for n in range(count)] + [row, column]
    spread = jnp.concatenate([(chosen * line).astype(BF16) for line in lines], axis=0)
    packed = lax.dot_general(spread, places, (((1,), (1,)), ((), ())), preferred_element_type=F32)

    def part(index):
        return packed[index * tiles:(index + 1) * tiles]

    send_ref[...] = jnp.zeros(send_ref.shape, F32)
    for n in range(count):
        send_ref[:, n, :CAP] = part(n) + (part(count + n) + part(2 * count + n))
    send_ref[:, count, :CAP] = part(3 * count)
    send_ref[:, count + 1, :CAP] = part(3 * count + 1)


def exchange(tiles, tracer, east, kappa, depth, top, send,
             west_tracer, west_speed, west_kappa, west_depth, east_tracer, east_kappa, east_depth,
             mirror, mirror_depth, received, out_sems, in_sems, pair_out, pair_in, own_sem):
    me = lax.axis_index("lon")
    right = lax.rem(me + 1, tiles)
    left = lax.rem(me + tiles - 1, tiles)
    partner = tiles - 1 - me
    last = tracer.shape[1] - 1
    barrier = pltpu.get_barrier_semaphore()

    @pl.loop(1, tiles)
    def _(step):
        pl.semaphore_signal(barrier, inc=1, device_id={"lon": lax.rem(me + step, tiles)},
                            device_id_type=pl.DeviceIdType.MESH)

    pl.semaphore_wait(barrier, tiles - 1)
    plan = [
        (top, mirror, partner),
        (depth, mirror_depth, partner),
        (tracer.at[:, last], west_tracer, right),
        (east.at[last], west_speed, right),
        (kappa.at[last], west_kappa, right),
        (depth, west_depth, right),
        (tracer.at[:, 0], east_tracer, left),
        (kappa.at[0], east_kappa, left),
        (depth, east_depth, left),
    ]
    copies = []
    for index, (source, target, device) in enumerate(plan):
        copies.append(pltpu.make_async_remote_copy(
            src_ref=source, dst_ref=target, send_sem=out_sems.at[index],
            recv_sem=in_sems.at[index], device_id={"lon": device},
            device_id_type=pl.DeviceIdType.MESH))
        copies[-1].start()

    def pair(to, arriving):
        return pltpu.make_async_remote_copy(
            src_ref=send.at[to], dst_ref=received.at[me], send_sem=pair_out.at[to],
            recv_sem=pair_in.at[arriving], device_id={"lon": to},
            device_id_type=pl.DeviceIdType.MESH)

    @pl.loop(1, tiles)
    def _(step):
        pair(lax.rem(me + step, tiles), me).start()

    own = pltpu.make_async_copy(send.at[me], received.at[me], own_sem)
    own.start()
    own.wait()
    for copy in copies:
        copy.wait()

    @pl.loop(1, tiles)
    def _(step):
        other = lax.rem(me + step, tiles)
        pltpu.make_async_remote_copy(
            src_ref=send.at[other], dst_ref=received.at[other], send_sem=pair_out.at[other],
            recv_sem=pair_in.at[other], device_id={"lon": other},
            device_id_type=pl.DeviceIdType.MESH).wait()


def advance(tracer, east, north, kappa, mixing, thickness, depth,
            west_tracer, west_speed, west_kappa, west_depth, east_tracer, east_kappa, east_depth,
            mirror, mirror_depth, received, out, values, thick, blend, gains):
    count, lon_cells, levels = tracer.shape[:3]
    tiles = received.shape[0]
    last = lon_cells - 1

    surface = jnp.zeros((3 * count * lon_cells, LANES), F32)
    for s in range(tiles):
        rows = received[s]
        hit = iota((lon_cells, LANES), 0).astype(F32) == rows[count:count + 1]
        lines = [p[n:n + 1] for p in thirds(rows[:count]) for n in range(count)]
        spread = jnp.concatenate(
            [jnp.where(hit, line, 0.0).astype(BF16) for line in lines], axis=0)
        spots = (iota((LANES, LANES), 0).astype(F32) == rows[count + 1:count + 2]).astype(F32)
        surface = surface + lax.dot_general(
            spread, spots.astype(BF16), (((1,), (1,)), ((), ())), preferred_element_type=F32)

    def flux_of(n):
        block = [surface[(p * count + n) * lon_cells:(p * count + n + 1) * lon_cells]
                 for p in range(3)]
        return block[0] + (block[1] + block[2])

    def weights(speed, near, far, open_face):
        half = 0.5 * (near + far)
        return (jnp.where(open_face, jnp.maximum(speed, 0.0) + half, 0.0),
                jnp.where(open_face, jnp.minimum(speed, 0.0) - half, 0.0))

    for start in range(0, levels, ROWS):
        size = min(ROWS, levels - start)
        ks = pl.ds(start, size)
        level = iota((size, LANES), 0) + start
        lane = iota((size, LANES), 1)
        at_fold = lane == LANES - 1
        row_fold = iota((1, LANES), 1) == LANES - 1

        def cell(i, east_far, kappa_far, depth_far, flux_before):
            here = [tracer[n, i, ks, :] for n in range(count)]
            kappa_here = kappa[i, ks, :]
            depth_here = depth[pl.ds(i, 1), :]
            ea, eb = weights(east[i, ks, :], kappa_here, kappa_far,
                             level < jnp.minimum(depth_here, depth_far))

            def beyond(x, f):
                other = pltpu.roll(mirror[ks, :], LANES - 1 - f * lon_cells - (last - i), 1)
                return jnp.where(at_fold, other, pltpu.roll(x, LANES - 1, 1))

            speed = north[i, ks, :]
            speed_far = pltpu.roll(mirror[ks, :], LANES - 1 - count * lon_cells - (last - i), 1)
            speed = jnp.where(at_fold, 0.5 * (speed - speed_far), speed)
            depth_north = jnp.where(row_fold, mirror_depth[pl.ds(last - i, 1), :],
                                    pltpu.roll(depth_here, LANES - 1, 1))
            na, nb = weights(speed, kappa_here, beyond(kappa_here, count + 1),
                             level < jnp.minimum(depth_here, depth_north))
            layer = thickness[i, ks, :]
            spots = pl.ds(start * lon_cells + i, size, stride=lon_cells)
            thick[spots, :] = layer
            blend[spots, :] = mixing[i, ks, :]
            fluxes = []
            for n in range(count):
                flux = ea * here[n] + eb * east_far[n]
                up = na * here[n] + nb * beyond(here[n], n)
                down = jnp.where(lane == 0, 0.0, pltpu.roll(up, 1, 1))
                stepped = (here[n] - (flux - flux_before[n])) - (up - down)
                values[n, spots, :] = layer * stepped
                fluxes.append(flux)
            return tuple(fluxes)

        wa, wb = weights(west_speed[ks, :], west_kappa[ks, :], kappa[0, ks, :],
                         level < jnp.minimum(west_depth[last:last + 1, :], depth[0:1, :]))
        before = tuple(wa * west_tracer[n, ks, :] + wb * tracer[n, 0, ks, :] for n in range(count))

        def inner(i, flux_before):
            return cell(i, [tracer[n, i + 1, ks, :] for n in range(count)], kappa[i + 1, ks, :],
                        depth[pl.ds(i + 1, 1), :], flux_before)

        before = lax.fori_loop(0, last, inner, before, unroll=3)
        cell(last, [east_tracer[n, ks, :] for n in range(count)], east_kappa[ks, :],
             east_depth[0:1, :], before)

    depths = depth[...]

    def at(k):
        return pl.ds(pl.multiple_of(k * lon_cells, lon_cells), lon_cells)

    def coupled(k, here, below):
        return jnp.where(depths > k + 1, blend[at(k), :] / (0.5 * (here + below)), 0.0)

    here = thick[at(0), :]
    below = thick[at(1), :]
    coupling = coupled(0, here, below)
    scale = 1.0 / (here + coupling)
    gain = coupling * scale
    gains[at(0), :] = gain
    value = []
    for n in range(count):
        value.append((values[n, at(0), :] + jnp.where(depths > 0, flux_of(n), 0.0)) * scale)
        values[n, at(0), :] = value[n]

    def down(k, state):
        here, prior, gain, value = state
        below = thick[at(k + 1), :]
        coupling = coupled(k, here, below)
        scale = 1.0 / (here + coupling + prior - prior * gain)
        gain = coupling * scale
        gains[at(k), :] = gain
        value = tuple((values[n, at(k), :] + prior * value[n]) * scale for n in range(count))
        for n in range(count):
            values[n, at(k), :] = value[n]
        return below, coupling, gain, value

    here, prior, gain, value = lax.fori_loop(
        1, levels - 1, down, (below, coupling, gain, tuple(value)), unroll=4)
    scale = 1.0 / (here + prior - prior * gain)
    solved = []
    for n in range(count):
        solved.append((values[n, at(levels - 1), :] + prior * value[n]) * scale)
        values[n, at(levels - 1), :] = solved[n]

    def up(step, solved):
        k = levels - 2 - step
        gain = gains[at(k), :]
        solved = tuple(values[n, at(k), :] + gain * solved[n] for n in range(count))
        for n in range(count):
            values[n, at(k), :] = solved[n]
        return solved

    lax.fori_loop(0, levels - 1, up, tuple(solved), unroll=4)

    @pl.loop(0, lon_cells)
    def _(i):
        for n in range(count):
            out[n, i] = values[n, pl.ds(i, levels, stride=lon_cells), :]


def shards(tracer, east_speed, north_speed, diffusivity, mixing, thickness, depth_levels,
           air_flux, margin_tile, margin_source, margin_cell, margin_weight):
    count, lon_cells, levels, lat_cells = tracer.shape
    tiles = lax.axis_size("lon")
    records = margin_source.shape[0]
    assert lat_cells == LANES and (count + 2) * lon_cells <= LANES
    shape = jax.ShapeDtypeStruct
    vmem = pl.BlockSpec(memory_space=pltpu.VMEM)
    left_in_place = pl.BlockSpec(memory_space=pl.ANY)
    big = pltpu.CompilerParams(vmem_limit_bytes=48 << 20)

    top, send = pl.pallas_call(
        lambda *refs: prepare(tiles, *refs),
        out_shape=(shape((levels, LANES), F32), shape((tiles, 8, LANES), F32)),
        in_specs=[vmem] * 8, out_specs=(vmem, vmem), compiler_params=big, name="prepare",
    )(margin_tile.reshape(1, records), margin_source.reshape(1, records),
      margin_cell.reshape(1, records), margin_weight.reshape(1, records), air_flux,
      tracer, north_speed, diffusivity)

    column = shape((levels, LANES), F32)
    stack = shape((count, levels, LANES), F32)
    depths = shape((lon_cells, LANES), I32)
    arrived = pl.pallas_call(
        lambda *refs: exchange(tiles, *refs),
        out_shape=(stack, column, column, depths, stack, column, depths, column, depths,
                   shape((tiles, 8, LANES), F32)),
        in_specs=[left_in_place] * 6, out_specs=(left_in_place,) * 10,
        scratch_shapes=[pltpu.SemaphoreType.DMA((9,)), pltpu.SemaphoreType.DMA((9,)),
                        pltpu.SemaphoreType.DMA((tiles,)), pltpu.SemaphoreType.DMA((tiles,)),
                        pltpu.SemaphoreType.DMA],
        compiler_params=pltpu.CompilerParams(collective_id=0, has_side_effects=True),
        name="exchange",
    )(tracer, east_speed, diffusivity, depth_levels, top, send)

    flat = (levels * lon_cells, LANES)
    return pl.pallas_call(
        advance,
        out_shape=shape(tracer.shape, F32),
        in_specs=[vmem] * 17, out_specs=vmem,
        scratch_shapes=[pltpu.VMEM((count, *flat), F32), pltpu.VMEM(flat, F32),
                        pltpu.VMEM(flat, F32), pltpu.VMEM(flat, F32)],
        compiler_params=big, name="advance",
    )(tracer, east_speed, north_speed, diffusivity, mixing, thickness, depth_levels, *arrived)


def solution(mesh):
    placed = (
        P(None, "lon", None, "ens"),
        P("lon", None, "ens"),
        P("lon", None, "ens"),
        P("lon", None, "ens"),
        P("lon", None, "ens"),
        P("lon", None, "ens"),
        P("lon", "ens"),
        P("ens", "lon"),
        P(("ens", "lon"), None),
        P(("ens", "lon")),
        P(("ens", "lon")),
        P(("ens", "lon")),
    )
    return jax.shard_map(
        shards, mesh=mesh, in_specs=placed, out_specs=P(None, "lon", None, "ens"), check_vma=False
    )
```

time: 144 us -> 55.6 us (0.39)
  other arithmetic: 72.8 us -> 0 us
  Pallas kernels: 0 us -> 30.2 us
  starting transfers between devices: 20.3 us -> 0 us
  local copies, waits for them, and re-layouts: 42 us -> 24.3 us
  waiting for transfers between devices: 4.13 us -> 0 us
  between operations: 2.83 us -> 0.2 us
    pallas_call x0 -> x3, Pallas kernels: none -> 30.2 us  [the longest x1 14.8 us: shards(): pl.pallas_call(lambda *refs: exchange(tiles, *refs), out_shape=(stack, co...]
    slice x20 -> x0, local copies, waits for them, and re-layouts: 15.2 us -> none  [the longest x2 4.85 us: shards(): tracer[:, :, :, -1]]
    mul x7 -> x0, other arithmetic: 12.9 us -> none  [the longest x3 6.84 us: face_flux(): open_face * (jnp.maximum(speed, 0.0) * near + jnp.minimum(speed, 0.0) * f...]
    sub x14 -> x0, other arithmetic: 12.6 us -> none  [the longest x13 9.39 us: mix_columns(): here_thickness + here_coupling + prior_coupling]
    unnamed x349 -> x66, local copies, waits for them, and re-layouts: 7.9 us -> 20.4 us
    ppermute x6 -> x0, starting transfers between devices: 11.4 us -> none  [the longest x4 5.91 us: from_partner(): return lax.ppermute(block, axis, route)]
    unnamed x40 -> x0, other arithmetic: 10.3 us -> none
    all_to_all x2 -> x0, starting transfers between devices: 8.91 us -> none  [the longest x1 4.71 us: shards(): lax.all_to_all(values, 'lon', split_axis=1, concat_axis=1, tiled=True)]
  transfers between devices with their start and end apart: 8 -> 0, of which waited for: 2 -> 0; matrix products, arithmetic and copies ran while one was open for 54% -> 0% of each run, Pallas kernels for 0% -> 0%
where the time goes in v1:
time: 55.6 us; the launch traced here: 54.7 us
  Pallas kernels  30.2 us (54%)
  local copies, waits for them, and re-layouts  24.3 us (44%)
    unnamed x66, local copies, waits for them, and re-layouts  20.4 us
    pallas_call x1, Pallas kernels, shards(): pl.pallas_call(lambda *refs: exchange(tiles, *refs), out_shape=(stack, co...  14.8 us
    pallas_call x1, Pallas kernels, shards(): pl.pallas_call(advance, out_shape=shape(tracer.shape, F32), in_specs=[vme...  12.9 us
    pallas_call x1, local copies, waits for them, and re-layouts, shards(): pl.pallas_call(advance, out_shape=shape(tracer.shape, F32), in_specs=[vme...  3.93 us
    pallas_call x1, Pallas kernels, shards(): pl.pallas_call(lambda *refs: prepare(tiles, *refs), out_shape=(shape((lev...  2.6 us

profile of v1, /device:TPU:0, one launch (start us, length us, event | category | flops | bytes accessed | tf_op | source)
XLA Modules:
  0.0 54.7 jit_solution(16426918714942837527)
XLA Ops:
  0.0 1.4 %copy.22.refs_7_.refs_2_.kappa = f32[16,75,128]{2,1,0:T(8,128)S(1)} copy(f32[16,75,128]{2,0,1:T(8,128)} %param.15) | data formatting | bytes 1228800 | tf_op args[3]
  1.4 2.4 %copy.20.refs_1_.east = f32[16,75,128]{2,1,0:T(8,128)} copy(f32[16,75,128]{2,0,1:T(8,128)} %param.13) | data formatting | bytes 1228800 | tf_op args[1]
  4.1 1.1 %copy.23.mixing = f32[16,75,128]{2,1,0:T(8,128)} copy(f32[16,75,128]{2,0,1:T(8,128)S(1)} %copy-done.28) | data formatting | bytes 1228800 | tf_op args[4]
  5.1 1.0 %copy.24.thickness = f32[16,75,128]{2,1,0:T(8,128)} copy(f32[16,75,128]{2,0,1:T(8,128)S(1)} %copy-done.29) | data formatting | bytes 1228800 | tf_op args[5]
  6.2 0.8 %copy.19.refs_5_.refs_0_.tracer = f32[4,16,75,128]{3,2,1,0:T(8,128)S(1)} copy(f32[4,16,75,128]{3,1,2,0:T(8,128)S(1)} %copy-done.26) | data formatting | bytes 4915200 | tf_op args[0]
  7.1 2.6 %prepare.1 = (f32[75,128]{1,0:T(8,128)S(1)}, f32[16,8,128]{2,1,0:T(8,128)S(1)}) custom-call(s32[1,1024]{1,0:T(1,128)S(1)} %bitcast.4, s32[1,1024]{1,0:T(1,128)S(1)} %bitcast.5, s32[1,1024]{1,0:T(1,128)S(1)} %bitcast.6, f32[1,1024]{1,0:T(1,128)S(1)} %bitcast.7, f32[4,256]{1,0:T(4,128)S(1)} %copy-done.25, f32[4,16,75,128]{3,2,1,0:T(8,128)S(1)} %copy.19.refs_5_.refs_0_.tracer, ...), custom_call_target="tpu_custom_call" | custom-call | tf_op jit(solution)/shard_map/prepare/pallas_call | solution.py:284
  9.7 0.6 %copy-done.11 = f32[16,8,128]{2,1,0:T(8,128)} copy-done((f32[16,8,128]{2,1,0:T(8,128)}, f32[16,8,128]{2,1,0:T(8,128)S(1)}, u32[]{:S(2)}) %copy-start.11) | copy-done | bytes 65560
  10.9 14.8 %exchange.1 = (f32[4,75,128]{2,1,0:T(8,128)}, f32[75,128]{1,0:T(8,128)}, f32[75,128]{1,0:T(8,128)}, s32[16,128]{1,0:T(8,128)}, f32[4,75,128]{2,1,0:T(8,128)}, /*...) custom-call(f32[4,16,75,128]{3,2,1,0:T(8,128)} %copy-done, ...), custom_call_target="tpu_custom_call" | custom-call | tf_op jit(solution)/shard_map/exchange/pallas_call | solution.py:295
  25.7 1.1 %copy-done.4 = f32[16,75,128]{2,1,0:T(8,128)S(1)} copy-done((f32[16,75,128]{2,1,0:T(8,128)S(1)}, f32[16,75,128]{2,1,0:T(8,128)}, u32[]{:S(2)}) %copy-start.4) | copy-done | bytes 614424
  26.8 1.1 %copy-done.5 = f32[16,75,128]{2,1,0:T(8,128)S(1)} copy-done((f32[16,75,128]{2,1,0:T(8,128)S(1)}, f32[16,75,128]{2,1,0:T(8,128)}, u32[]{:S(2)}) %copy-start.5) | copy-done | bytes 614424
  27.9 1.1 %copy-done.6 = f32[16,75,128]{2,1,0:T(8,128)S(1)} copy-done((f32[16,75,128]{2,1,0:T(8,128)S(1)}, f32[16,75,128]{2,1,0:T(8,128)}, u32[]{:S(2)}) %copy-start.6) | copy-done | bytes 614424
  28.9 1.1 %copy-done.7 = f32[16,75,128]{2,1,0:T(8,128)S(1)} copy-done((f32[16,75,128]{2,1,0:T(8,128)S(1)}, f32[16,75,128]{2,1,0:T(8,128)}, u32[]{:S(2)}) %copy-start.7) | copy-done | bytes 614424
  30.0 0.9 %copy-done.8 = f32[4,75,128]{2,1,0:T(8,128)S(1)} copy-done((f32[4,75,128]{2,1,0:T(8,128)S(1)}, f32[4,75,128]{2,1,0:T(8,128)}, u32[]{:S(2)}) %copy-start.8) | copy-done | bytes 153624
  31.0 0.9 %copy-done.9 = f32[4,75,128]{2,1,0:T(8,128)S(1)} copy-done((f32[4,75,128]{2,1,0:T(8,128)S(1)}, f32[4,75,128]{2,1,0:T(8,128)}, u32[]{:S(2)}) %copy-start.9) | copy-done | bytes 153624
  31.9 0.8 %copy-done.10 = f32[16,8,128]{2,1,0:T(8,128)S(1)} copy-done((f32[16,8,128]{2,1,0:T(8,128)S(1)}, f32[16,8,128]{2,1,0:T(8,128)}, u32[]{:S(2)}) %copy-start.10) | copy-done | bytes 65560
  32.7 0.8 %copy-done.13 = f32[75,128]{1,0:T(8,128)S(1)} copy-done((f32[75,128]{1,0:T(8,128)S(1)}, f32[75,128]{1,0:T(8,128)}, u32[]{:S(2)}) %copy-start.13) | copy-done | bytes 38424
  33.5 0.8 %copy-done.14 = f32[75,128]{1,0:T(8,128)S(1)} copy-done((f32[75,128]{1,0:T(8,128)S(1)}, f32[75,128]{1,0:T(8,128)}, u32[]{:S(2)}) %copy-start.14) | copy-done | bytes 38424
  34.3 0.8 %copy-done.15 = f32[75,128]{1,0:T(8,128)S(1)} copy-done((f32[75,128]{1,0:T(8,128)S(1)}, f32[75,128]{1,0:T(8,128)}, u32[]{:S(2)}) %copy-start.15) | copy-done | bytes 38424
  35.0 0.8 %copy-done.16 = f32[75,128]{1,0:T(8,128)S(1)} copy-done((f32[75,128]{1,0:T(8,128)S(1)}, f32[75,128]{1,0:T(8,128)}, u32[]{:S(2)}) %copy-start.16) | copy-done | bytes 38424
  35.8 0.7 %copy-done.18 = s32[16,128]{1,0:T(8,128)S(1)} copy-done((s32[16,128]{1,0:T(8,128)S(1)}, s32[16,128]{1,0:T(8,128)}, u32[]{:S(2)}) %copy-start.18) | copy-done | bytes 8216
  36.5 0.7 %copy-done.19 = s32[16,128]{1,0:T(8,128)S(1)} copy-done((s32[16,128]{1,0:T(8,128)S(1)}, s32[16,128]{1,0:T(8,128)}, u32[]{:S(2)}) %copy-start.19) | copy-done | bytes 8216
  37.2 0.7 %copy-done.20 = s32[16,128]{1,0:T(8,128)S(1)} copy-done((s32[16,128]{1,0:T(8,128)S(1)}, s32[16,128]{1,0:T(8,128)}, u32[]{:S(2)}) %copy-start.20) | copy-done | bytes 8216
  37.9 12.9 %advance.1 = f32[4,16,75,128]{3,2,1,0:T(8,128)} custom-call(f32[4,16,75,128]{3,2,1,0:T(8,128)} %copy-done, f32[16,75,128]{2,1,0:T(8,128)S(1)} %copy-done.5, f32[16,75,128]{2,1,0:T(8,128)S(1)} %copy-done.4, f32[16,75,128]{2,1,0:T(8,128)S(1)} %copy-done.2, f32[16,75,128]{2,1,0:T(8,128)S(1)} %copy-done.6, f32[16,75,128]{2,1,0:T(8,128)S(1)} %copy-done.7, ...), custom_call_target="tpu_custom_call" | custom-call | tf_op jit(solution)/shard_map/advance/pallas_call | solution.py:308
  50.8 3.9 %copy.25 = f32[4,16,75,128]{3,1,2,0:T(8,128)} copy(f32[4,16,75,128]{3,2,1,0:T(8,128)} %advance.1) | data formatting | bytes 4915200 | tf_op jit(solution)/shard_map/advance/pallas_call | solution.py:308
  (46 shorter events, 0.9 us)
Async XLA Ops:
  0.0 5.1 %copy-start.29 = (f32[16,75,128]{2,0,1:T(8,128)S(1)}, f32[16,75,128]{2,0,1:T(8,128)}, u32[]{:S(2)}) copy-start(f32[16,75,128]{2,0,1:T(8,128)} %param.17) | copy-start | bytes 1843204
  0.0 4.0 %copy-start.28 = (f32[16,75,128]{2,0,1:T(8,128)S(1)}, f32[16,75,128]{2,0,1:T(8,128)}, u32[]{:S(2)}) copy-start(f32[16,75,128]{2,0,1:T(8,128)} %param.16) | copy-start | bytes 1843204
  0.0 3.8 %copy-start.27 = (f32[16,75,128]{2,0,1:T(8,128)S(1)}, f32[16,75,128]{2,0,1:T(8,128)}, u32[]{:S(2)}) copy-start(f32[16,75,128]{2,0,1:T(8,128)} %param.14) | copy-start | bytes 1843204
  1.4 5.6 %copy-start.1 = (f32[16,75,128]{2,1,0:T(8,128)}, f32[16,75,128]{2,1,0:T(8,128)S(1)}, u32[]{:S(2)}) copy-start(f32[16,75,128]{2,1,0:T(8,128)S(1)} %copy.22.refs_7_.refs_2_.kappa) | copy-start | bytes 1843204
  1.4 4.7 %copy-start.26 = (f32[4,16,75,128]{3,1,2,0:T(8,128)S(1)}, f32[4,16,75,128]{3,1,2,0:T(8,128)}, u32[]{:S(2)}) copy-start(f32[4,16,75,128]{3,1,2,0:T(8,128)} %param.12) | copy-start | bytes 7372804
  4.0 2.9 %copy-start.3 = (f32[16,75,128]{2,1,0:T(8,128)}, f32[16,75,128]{2,1,0:T(8,128)S(1)}, u32[]{:S(2)}) copy-start(f32[16,75,128]{2,1,0:T(8,128)S(1)} %copy.21.refs_6_.north) | copy-start | bytes 1843204
  6.2 0.8 %copy-start.21 = (s32[1024,1]{0,1:T(1,128)S(1)}, s32[1024,1]{0,1:T(1,128)}, u32[]{:S(2)}) copy-start(s32[1024,1]{0,1:T(1,128)} %param.20) | copy-start | bytes 12292
  6.2 0.8 %copy-start.22 = (s32[1024]{0:T(1024)S(1)}, s32[1024]{0:T(1024)}, u32[]{:S(2)}) copy-start(s32[1024]{0:T(1024)} %param.21) | copy-start | bytes 12292
  6.2 0.9 %copy-start.23 = (s32[1024]{0:T(1024)S(1)}, s32[1024]{0:T(1024)}, u32[]{:S(2)}) copy-start(s32[1024]{0:T(1024)} %param.22) | copy-start | bytes 12292
  6.2 0.9 %copy-start.24 = (f32[1024]{0:T(1024)S(1)}, f32[1024]{0:T(1024)}, u32[]{:S(2)}) copy-start(f32[1024]{0:T(1024)} %param.23) | copy-start | bytes 12292
  6.2 0.9 %copy-start.25 = (f32[4,256]{1,0:T(4,128)S(1)}, f32[4,256]{1,0:T(4,128)}, u32[]{:S(2)}) copy-start(f32[4,256]{1,0:T(4,128)} %refs_4_.1) | copy-start | bytes 12292
  7.0 3.9 %copy-start = (f32[4,16,75,128]{3,2,1,0:T(8,128)}, f32[4,16,75,128]{3,2,1,0:T(8,128)S(1)}, u32[]{:S(2)}) copy-start(f32[4,16,75,128]{3,2,1,0:T(8,128)S(1)} %copy.19.refs_5_.refs_0_.tracer) | copy-start | bytes 7372804
  10.9 14.8 %copy-start.2 = (f32[16,75,128]{2,1,0:T(8,128)S(1)}, f32[16,75,128]{2,1,0:T(8,128)}, u32[]{:S(2)}) copy-start(f32[16,75,128]{2,1,0:T(8,128)} %copy-done.1) | copy-start | bytes 1843204
  10.9 14.8 %copy-start.17 = (s32[16,128]{1,0:T(8,128)S(1)}, s32[16,128]{1,0:T(8,128)}, u32[]{:S(2)}) copy-start(s32[16,128]{1,0:T(8,128)} %depth.1) | copy-start | bytes 24580
  25.7 1.1 %copy-start.4 = (f32[16,75,128]{2,1,0:T(8,128)S(1)}, f32[16,75,128]{2,1,0:T(8,128)}, u32[]{:S(2)}) copy-start(f32[16,75,128]{2,1,0:T(8,128)} %copy-done.3) | copy-start | bytes 1843204
  26.8 1.1 %copy-start.5 = (f32[16,75,128]{2,1,0:T(8,128)S(1)}, f32[16,75,128]{2,1,0:T(8,128)}, u32[]{:S(2)}) copy-start(f32[16,75,128]{2,1,0:T(8,128)} %copy.20.refs_1_.east) | copy-start | bytes 1843204
  27.9 1.1 %copy-start.6 = (f32[16,75,128]{2,1,0:T(8,128)S(1)}, f32[16,75,128]{2,1,0:T(8,128)}, u32[]{:S(2)}) copy-start(f32[16,75,128]{2,1,0:T(8,128)} %copy.23.mixing) | copy-start | bytes 1843204
  28.9 1.1 %copy-start.7 = (f32[16,75,128]{2,1,0:T(8,128)S(1)}, f32[16,75,128]{2,1,0:T(8,128)}, u32[]{:S(2)}) copy-start(f32[16,75,128]{2,1,0:T(8,128)} %copy.24.thickness) | copy-start | bytes 1843204
  30.0 0.9 %copy-start.8 = (f32[4,75,128]{2,1,0:T(8,128)S(1)}, f32[4,75,128]{2,1,0:T(8,128)}, u32[]{:S(2)}) copy-start(f32[4,75,128]{2,1,0:T(8,128)} %get-tuple-element.19.west_tracer) | copy-start | bytes 460804
  31.0 0.9 %copy-start.9 = (f32[4,75,128]{2,1,0:T(8,128)S(1)}, f32[4,75,128]{2,1,0:T(8,128)}, u32[]{:S(2)}) copy-start(f32[4,75,128]{2,1,0:T(8,128)} %get-tuple-element.23.east_tracer) | copy-start | bytes 460804
  31.9 0.8 %copy-start.10 = (f32[16,8,128]{2,1,0:T(8,128)S(1)}, f32[16,8,128]{2,1,0:T(8,128)}, u32[]{:S(2)}) copy-start(f32[16,8,128]{2,1,0:T(8,128)} %get-tuple-element.28.received) | copy-start | bytes 196612
  32.7 0.8 %copy-start.13 = (f32[75,128]{1,0:T(8,128)S(1)}, f32[75,128]{1,0:T(8,128)}, u32[]{:S(2)}) copy-start(f32[75,128]{1,0:T(8,128)} %get-tuple-element.20.west_speed) | copy-start | bytes 115204
  33.5 0.8 %copy-start.14 = (f32[75,128]{1,0:T(8,128)S(1)}, f32[75,128]{1,0:T(8,128)}, u32[]{:S(2)}) copy-start(f32[75,128]{1,0:T(8,128)} %get-tuple-element.21.west_kappa) | copy-start | bytes 115204
  34.3 0.8 %copy-start.15 = (f32[75,128]{1,0:T(8,128)S(1)}, f32[75,128]{1,0:T(8,128)}, u32[]{:S(2)}) copy-start(f32[75,128]{1,0:T(8,128)} %get-tuple-element.24.east_kappa) | copy-start | bytes 115204
  (6 other events, 4.1 us)

commit v2 on v0

v2 whole, which is shorter than its diff:
```python
import jax
import jax.numpy as jnp
from jax import lax
from jax.experimental import pallas as pl
from jax.experimental.pallas import tpu as pltpu
from jax.sharding import PartitionSpec as P

CAP = 64
LANES = 128
F32 = jnp.float32
BF16 = jnp.bfloat16
I32 = jnp.int32


def iota(shape, axis):
    return lax.broadcasted_iota(I32, shape, axis)


def thirds(x):
    high = x.astype(BF16).astype(F32)
    rest = x - high
    middle = rest.astype(BF16).astype(F32)
    return high, middle, rest - middle


def route(tiles, tile, source, cells, weight, air, send_ref):
    count, air_cells = air.shape
    records = tile.shape[1]
    picks = (iota((air_cells, records), 0) == source).astype(F32).astype(BF16)
    parts = jnp.concatenate(thirds(air), axis=0).astype(BF16)
    found = jnp.dot(parts, picks, preferred_element_type=F32)
    found = found[:count] + (found[count:2 * count] + found[2 * count:])
    payload = weight * found

    chosen = (iota((tiles, records), 0) == tile).astype(F32)
    earlier = (iota((LANES, LANES), 0) < iota((LANES, LANES), 1)).astype(F32).astype(BF16)
    carried = jnp.zeros((tiles, 1), F32)
    slots = []
    for start in range(0, records, LANES):
        piece = chosen[:, start:start + LANES]
        rank = jnp.dot(piece.astype(BF16), earlier, preferred_element_type=F32) + carried
        slots.append(jnp.sum(piece * rank, axis=0, keepdims=True))
        carried = carried + jnp.sum(piece, axis=1, keepdims=True)
    slot = jnp.concatenate(slots, axis=1)
    places = (iota((CAP, records), 0).astype(F32) == slot).astype(F32).astype(BF16)

    row = (cells >> 7).astype(F32)
    column = (cells & (LANES - 1)).astype(F32)
    lines = [p[n:n + 1] for p in thirds(payload) for n in range(count)] + [row, column]
    spread = jnp.concatenate([(chosen * line).astype(BF16) for line in lines], axis=0)
    packed = lax.dot_general(spread, places, (((1,), (1,)), ((), ())), preferred_element_type=F32)

    def part(index):
        return packed[index * tiles:(index + 1) * tiles]

    send_ref[...] = jnp.zeros(send_ref.shape, F32)
    for n in range(count):
        send_ref[:, n, :CAP] = part(n) + (part(count + n) + part(2 * count + n))
    send_ref[:, count, :CAP] = part(3 * count)
    send_ref[:, count + 1, :CAP] = part(3 * count + 1)


def gathered(received, count, lon_cells):
    surface = jnp.zeros((3 * count * lon_cells, LANES), F32)
    for s in range(received.shape[0]):
        rows = received[s]
        hit = iota((lon_cells, LANES), 0).astype(F32) == rows[count:count + 1]
        lines = [p[n:n + 1] for p in thirds(rows[:count]) for n in range(count)]
        spread = jnp.concatenate(
            [jnp.where(hit, line, 0.0).astype(BF16) for line in lines], axis=0)
        spots = (iota((LANES, LANES), 0).astype(F32) == rows[count + 1:count + 2]).astype(F32)
        surface = surface + lax.dot_general(
            spread, spots.astype(BF16), (((1,), (1,)), ((), ())), preferred_element_type=F32)
    fluxes = []
    for n in range(count):
        block = [surface[(p * count + n) * lon_cells:(p * count + n + 1) * lon_cells]
                 for p in range(3)]
        fluxes.append(block[0] + (block[1] + block[2]))
    return fluxes


def weights(speed, near, far, open_face):
    half = 0.5 * (near + far)
    return (jnp.where(open_face, jnp.maximum(speed, 0.0) + half, 0.0),
            jnp.where(open_face, jnp.minimum(speed, 0.0) - half, 0.0))


def step(tiles, *refs):
    sources, refs = refs[:12], refs[12:]
    out, refs = refs[0], refs[1:]
    held, refs = refs[:12], refs[12:]
    (values, gains, factor, share, top, fold_out, fold_in, right_out, right_in, left_out, left_in,
     send, received, load_sems, store_sems, out_sems, in_sems, pair_out, pair_in, own_sem) = refs
    (tracer, east, north, kappa, mixing, thickness, depth_ref, air, tile, source, cells,
     weight) = held
    count, planes = tracer.shape[:2]
    lon_cells = depth_ref.shape[0]
    levels = planes // lon_cells
    last = lon_cells - 1

    loads = [pltpu.make_async_copy(a, b, load_sems.at[i])
             for i, (a, b) in enumerate(zip(sources, held))]
    for i in (7, 8, 9, 10, 11, 0, 2, 3, 1, 6, 5, 4):
        loads[i].start()

    me = lax.axis_index("lon")
    right = lax.rem(me + 1, tiles)
    left = lax.rem(me + tiles - 1, tiles)
    partner = tiles - 1 - me
    barrier = pltpu.get_barrier_semaphore()

    @pl.loop(1, tiles)
    def _(hop):
        pl.semaphore_signal(barrier, inc=1, device_id={"lon": lax.rem(me + hop, tiles)},
                            device_id_type=pl.DeviceIdType.MESH)

    for i in (7, 8, 9, 10, 11):
        loads[i].wait()
    route(tiles, tile[...], source[...], cells[...], weight[...], air[...], send)

    for i in (0, 2, 3, 1, 6):
        loads[i].wait()
    depth = depth_ref[...]

    def at(k):
        return pl.ds(pl.multiple_of(k * lon_cells, lon_cells), lon_cells)

    def column(i):
        return pl.ds(i, levels, stride=lon_cells)

    for n in range(count):
        right_out[n, :levels, :] = tracer[n, column(last), :]
        left_out[n, :levels, :] = tracer[n, column(0), :]
    right_out[count, :levels, :] = kappa[column(last), :]
    left_out[count, :levels, :] = kappa[column(0), :]
    right_out[count + 1, :levels, :] = east[column(last), :]
    right_out[count, levels:levels + 1, :] = depth[last:, :].astype(F32)
    left_out[count, levels:levels + 1, :] = depth[:1, :].astype(F32)

    lane = iota((lon_cells, LANES), 1)

    def take(k, packed):
        fields = [tracer[n, at(k), :] for n in range(count)] + [kappa[at(k), :], north[at(k), :]]
        return tuple(jnp.where(lane == k, pltpu.roll(x, k + 1, 1), p)
                     for x, p in zip(fields, packed))

    empty = jnp.zeros((lon_cells, LANES), F32)
    packed = lax.fori_loop(0, levels, take, (empty,) * (count + 2), unroll=3)
    packed += (jnp.broadcast_to(depth[:, LANES - 1:].astype(F32), (lon_cells, LANES)),)
    for f, plane in enumerate(packed):
        top[f] = plane
        for i in range(lon_cells):
            fold_out[f, last - i:last - i + 1, :] = plane[i:i + 1]

    pl.semaphore_wait(barrier, tiles - 1)
    copies = []
    for index, (a, b, device) in enumerate([
            (right_out, right_in, right), (left_out, left_in, left), (fold_out, fold_in, partner)]):
        copies.append(pltpu.make_async_remote_copy(
            src_ref=a, dst_ref=b, send_sem=out_sems.at[index], recv_sem=in_sems.at[index],
            device_id={"lon": device}, device_id_type=pl.DeviceIdType.MESH))
        copies[-1].start()

    @pl.loop(1, tiles)
    def _(hop):
        other = lax.rem(me + hop, tiles)
        pltpu.make_async_remote_copy(
            src_ref=send.at[other], dst_ref=received.at[me], send_sem=pair_out.at[other],
            recv_sem=pair_in.at[me], device_id={"lon": other},
            device_id_type=pl.DeviceIdType.MESH).start()

    own = pltpu.make_async_copy(send.at[me], received.at[me], own_sem)
    own.start()
    for i in (5, 4):
        loads[i].wait()

    row = iota((lon_cells, LANES), 0)
    depth_east = jnp.where(row == last, 0, pltpu.roll(depth, last, 0))
    depth_north = jnp.where(lane == LANES - 1, 0, pltpu.roll(depth, LANES - 1, 1))
    open_east = jnp.minimum(depth, depth_east)
    open_north = jnp.minimum(depth, depth_north)

    def inner(k, state):
        prior, gain = state
        here = thickness[at(k), :]
        below = thickness[at(jnp.minimum(k + 1, levels - 1)), :]
        coupling = jnp.where(depth > k + 1, mixing[at(k), :] / (0.5 * (here + below)), 0.0)
        scale = 1.0 / (here + coupling + prior - prior * gain)
        gain = coupling * scale
        gains[at(k), :] = gain
        factor[at(k), :] = prior * scale
        part = here * scale
        share[at(k), :] = part
        spread = kappa[at(k), :]
        ea, eb = weights(east[at(k), :], spread, pltpu.roll(spread, last, 0), open_east > k)
        na, nb = weights(north[at(k), :], spread, pltpu.roll(spread, LANES - 1, 1), open_north > k)
        for n in range(count):
            t = tracer[n, at(k), :]
            zonal = ea * t + eb * pltpu.roll(t, last, 0)
            up = na * t + nb * pltpu.roll(t, LANES - 1, 1)
            stepped = (t - (zonal - pltpu.roll(zonal, 1, 0))) - (up - pltpu.roll(up, 1, 1))
            values[n, at(k), :] = part * stepped
        return coupling, gain

    lax.fori_loop(0, levels, inner, (empty, empty), unroll=3)

    for copy in copies:
        copy.wait()
    deep = iota((levels, LANES), 0)

    first_share = share[column(0), :]
    last_share = share[column(last), :]
    wa, wb = weights(right_in[count + 1, :levels, :], right_in[count, :levels, :],
                     kappa[column(0), :],
                     deep < jnp.minimum(right_in[count, levels:levels + 1, :].astype(I32), depth[:1]))
    ea, eb = weights(east[column(last), :], kappa[column(last), :], left_in[count, :levels, :],
                     deep < jnp.minimum(left_in[count, levels:levels + 1, :].astype(I32), depth[last:]))
    for n in range(count):
        flux = wa * right_in[n, :levels, :] + wb * tracer[n, column(0), :]
        values[n, column(0), :] = values[n, column(0), :] + first_share * flux
        flux = ea * tracer[n, column(last), :] + eb * left_in[n, :levels, :]
        values[n, column(last), :] = values[n, column(last), :] - last_share * flux
    fa, fb = weights(0.5 * (top[count + 1] - fold_in[count + 1]), top[count], fold_in[count],
                     lane < jnp.minimum(top[count + 2], fold_in[count + 2]).astype(I32))
    fold = [fa * top[n] + fb * fold_in[n] for n in range(count)]

    own.wait()

    @pl.loop(1, tiles)
    def _(hop):
        other = lax.rem(me + hop, tiles)
        pltpu.make_async_remote_copy(
            src_ref=send.at[other], dst_ref=received.at[other], send_sem=pair_out.at[other],
            recv_sem=pair_in.at[other], device_id={"lon": other},
            device_id_type=pl.DeviceIdType.MESH).wait()

    surface = gathered(received, count, lon_cells)
    pivot = share[at(0), :] / thickness[at(0), :]
    for n in range(count):
        values[n, at(0), :] = values[n, at(0), :] + jnp.where(depth > 0, surface[n] * pivot, 0.0)

    def down(k, value):
        part = jnp.where(lane == LANES - 1, share[at(k), :], 0.0)
        mult = factor[at(k), :]
        solved = []
        for n in range(count):
            own_part = values[n, at(k), :] - part * pltpu.roll(fold[n], LANES - 1 - k, 1)
            solved.append(own_part + mult * value[n])
            values[n, at(k), :] = solved[n]
        return tuple(solved)

    value = lax.fori_loop(0, levels, down, (empty,) * count, unroll=3)

    chunk = 15
    stores = []
    value = (empty,) * count
    for index, begin in enumerate(range(levels // chunk * chunk, -1, -chunk)):
        end = min(begin + chunk, levels)
        if begin == end:
            continue

        def up(move, value, end=end):
            k = end - 1 - move
            gain = gains[at(k), :]
            solved = tuple(values[n, at(k), :] + gain * value[n] for n in range(count))
            for n in range(count):
                values[n, at(k), :] = solved[n]
            return solved

        value = lax.fori_loop(0, end - begin, up, value, unroll=5)
        block = pl.ds(begin * lon_cells, (end - begin) * lon_cells)
        stores.append(pltpu.make_async_copy(
            values.at[:, block], out.at[:, block], store_sems.at[index]))
        stores[-1].start()
    for store in stores:
        store.wait()


def shards(tracer, east_speed, north_speed, diffusivity, mixing, thickness, depth_levels,
           air_flux, margin_tile, margin_source, margin_cell, margin_weight):
    count, lon_cells, levels, lat_cells = tracer.shape
    tiles = lax.axis_size("lon")
    records = margin_source.shape[0]
    assert lat_cells == LANES and levels < LANES

    def by_level(x):
        return x.transpose(1, 0, 2).reshape(levels * lon_cells, LANES)

    operands = (
        tracer.transpose(0, 2, 1, 3).reshape(count, levels * lon_cells, LANES),
        *[by_level(x) for x in (east_speed, north_speed, diffusivity, mixing, thickness)],
        depth_levels, air_flux,
        *[x.reshape(1, records) for x in (margin_tile, margin_source, margin_cell, margin_weight)])
    hbm = pl.BlockSpec(memory_space=pltpu.HBM)
    flat = pltpu.VMEM((levels * lon_cells, LANES), F32)
    rows = (levels + 8) // 8 * 8
    fold = pltpu.VMEM((count + 3, lon_cells, LANES), F32)
    pairs = pltpu.VMEM((tiles, 8, LANES), F32)
    dma = pltpu.SemaphoreType.DMA
    result = pl.pallas_call(
        lambda *refs: step(tiles, *refs),
        out_shape=jax.ShapeDtypeStruct(operands[0].shape, F32),
        in_specs=[hbm] * 12, out_specs=hbm,
        scratch_shapes=[pltpu.VMEM(x.shape, x.dtype) for x in operands] + [
            pltpu.VMEM(operands[0].shape, F32), flat, flat, flat, fold, fold, fold,
            pltpu.VMEM((count + 2, rows, LANES), F32), pltpu.VMEM((count + 2, rows, LANES), F32),
            pltpu.VMEM((count + 1, rows, LANES), F32), pltpu.VMEM((count + 1, rows, LANES), F32),
            pairs, pairs, dma((12,)), dma((levels // 15 + 1,)), dma((3,)), dma((3,)),
            dma((tiles,)), dma((tiles,)), dma],
        compiler_params=pltpu.CompilerParams(
            collective_id=0, has_side_effects=True, vmem_limit_bytes=60 << 20),
        name="ocean_step",
    )(*operands)
    return result.reshape(count, levels, lon_cells, LANES).transpose(0, 2, 1, 3)


def solution(mesh):
    placed = (
        P(None, "lon", None, "ens"),
        P("lon", None, "ens"),
        P("lon", None, "ens"),
        P("lon", None, "ens"),
        P("lon", None, "ens"),
        P("lon", None, "ens"),
        P("lon", "ens"),
        P("ens", "lon"),
        P(("ens", "lon"), None),
        P(("ens", "lon")),
        P(("ens", "lon")),
        P(("ens", "lon")),
    )
    return jax.shard_map(
        shards, mesh=mesh, in_specs=placed, out_specs=P(None, "lon", None, "ens"), check_vma=False
    )
```

time: 144 us -> 25.6 us (0.18); the launches traced: 142 us -> 25.4 us
  other arithmetic: 72.8 us -> 0 us
  local copies, waits for them, and re-layouts: 42 us -> 3.29 us
  Pallas kernels: 0 us -> 22.1 us
  starting transfers between devices: 20.3 us -> 0 us
  waiting for transfers between devices: 4.13 us -> 0 us
  between operations: 2.83 us -> 0.01 us
    pallas_call x0 -> x1, Pallas kernels: none -> 22.1 us  [shards(): pl.pallas_call(lambda *refs: step(tiles, *refs), out_shape=jax.ShapeDtype...]
    slice x20 -> x0, local copies, waits for them, and re-layouts: 15.2 us -> none  [the longest x2 4.85 us: shards(): tracer[:, :, :, -1]]
    mul x7 -> x0, other arithmetic: 12.9 us -> none  [the longest x3 6.84 us: face_flux(): open_face * (jnp.maximum(speed, 0.0) * near + jnp.minimum(speed, 0.0) * f...]
    sub x14 -> x0, other arithmetic: 12.6 us -> none  [the longest x13 9.39 us: mix_columns(): here_thickness + here_coupling + prior_coupling]
    ppermute x6 -> x0, starting transfers between devices: 11.4 us -> none  [the longest x4 5.91 us: from_partner(): return lax.ppermute(block, axis, route)]
    unnamed x40 -> x0, other arithmetic: 10.3 us -> none
    all_to_all x2 -> x0, starting transfers between devices: 8.91 us -> none  [the longest x1 4.71 us: shards(): lax.all_to_all(values, 'lon', split_axis=1, concat_axis=1, tiled=True)]
    scatter x1 -> x0, other arithmetic: 7.59 us -> none  [shards(): jnp.zeros((tracer_count, cycle_size * CAP), jnp.float32).at[:, position]]
  transfers between devices with their start and end apart: 8 -> 0, of which waited for: 2 -> 0; matrix products, arithmetic and copies ran while one was open for 54% -> 0% of each run, Pallas kernels for 0% -> 0%
where the time goes in v2:
time: 25.6 us; the launch traced here: 25.4 us
  Pallas kernels  22.1 us (86%)
  local copies, waits for them, and re-layouts  3.29 us (13%)
    pallas_call x1, Pallas kernels, shards(): pl.pallas_call(lambda *refs: step(tiles, *refs), out_shape=jax.ShapeDtype...  22.1 us
    unnamed x1, local copies, waits for them, and re-layouts  3.29 us

profile of v2, /device:TPU:0, one launch (start us, length us, event | category | flops | bytes accessed | tf_op | source)
XLA Modules:
  0.0 25.4 jit_solution(9517844079445800921)
XLA Ops:
  0.0 22.1 %ocean_step.1 = f32[4,1200,128]{2,1,0:T(8,128)} custom-call(f32[4,1200,128]{2,1,0:T(8,128)} %bitcast.26, f32[1200,128]{1,0:T(8,128)} %bitcast.27, f32[1200,128]{1,0:T(8,128)} %bitcast.28, f32[1200,128]{1,0:T(8,128)} %bitcast.29, f32[1200,128]{1,0:T(8,128)} %bitcast.30, f32[1200,128]{1,0:T(8,128)} %bitcast.31, s32[16,128]{1,0:T(8,128)} %refs_6_.1, ...), custom_call_target="tpu_custom_call" | custom-call | tf_op jit(solution)/shard_map/ocean_step/pallas_call | solution.py:300
  22.1 3.3 %copy.14 = f32[4,16,75,128]{3,1,2,0:T(8,128)} copy(f32[4,16,75,128]{3,1,2,0:T(8,128)} %bitcast.25) | data formatting | bytes 4915200

commit v3 on v2

--- a/solution.py
+++ b/solution.py
@@ -137,29 +137,18 @@
     right_out[count, levels:levels + 1, :] = depth[last:, :].astype(F32)
     left_out[count, levels:levels + 1, :] = depth[:1, :].astype(F32)
 
-    lane = iota((lon_cells, LANES), 1)
-
-    def take(k, packed):
-        fields = [tracer[n, at(k), :] for n in range(count)] + [kappa[at(k), :], north[at(k), :]]
-        return tuple(jnp.where(lane == k, pltpu.roll(x, k + 1, 1), p)
-                     for x, p in zip(fields, packed))
-
-    empty = jnp.zeros((lon_cells, LANES), F32)
-    packed = lax.fori_loop(0, levels, take, (empty,) * (count + 2), unroll=3)
-    packed += (jnp.broadcast_to(depth[:, LANES - 1:].astype(F32), (lon_cells, LANES)),)
-    for f, plane in enumerate(packed):
-        top[f] = plane
-        for i in range(lon_cells):
-            fold_out[f, last - i:last - i + 1, :] = plane[i:i + 1]
-
     pl.semaphore_wait(barrier, tiles - 1)
     copies = []
-    for index, (a, b, device) in enumerate([
-            (right_out, right_in, right), (left_out, left_in, left), (fold_out, fold_in, partner)]):
+
+    def start(a, b, device):
+        index = len(copies)
         copies.append(pltpu.make_async_remote_copy(
             src_ref=a, dst_ref=b, send_sem=out_sems.at[index], recv_sem=in_sems.at[index],
             device_id={"lon": device}, device_id_type=pl.DeviceIdType.MESH))
         copies[-1].start()
+
+    start(right_out, right_in, right)
+    start(left_out, left_in, left)
 
     @pl.loop(1, tiles)
     def _(hop):
@@ -169,6 +158,22 @@
             recv_sem=pair_in.at[me], device_id={"lon": other},
             device_id_type=pl.DeviceIdType.MESH).start()
 
+    lane = iota((lon_cells, LANES), 1)
+
+    def take(k, packed):
+        fields = [tracer[n, at(k), :] for n in range(count)] + [kappa[at(k), :], north[at(k), :]]
+        return tuple(jnp.where(lane == k, pltpu.roll(x, k + 1, 1), p)
+                     for x, p in zip(fields, packed))
+
+    empty = jnp.zeros((lon_cells, LANES), F32)
+    packed = lax.fori_loop(0, levels, take, (empty,) * (count + 2), unroll=15)
+    packed += (jnp.broadcast_to(depth[:, LANES - 1:].astype(F32), (lon_cells, LANES)),)
+    for f, plane in enumerate(packed):
+        top[f] = plane
+        for i in range(lon_cells):
+            fold_out[f, last - i:last - i + 1, :] = plane[i:i + 1]
+
+    start(fold_out, fold_in, partner)
     own = pltpu.make_async_copy(send.at[me], received.at[me], own_sem)
     own.start()
     for i in (5, 4):
@@ -249,7 +254,7 @@
             values[n, at(k), :] = solved[n]
         return tuple(solved)
 
-    value = lax.fori_loop(0, levels, down, (empty,) * count, unroll=3)
+    value = lax.fori_loop(0, levels, down, (empty,) * count, unroll=15)
 
     chunk = 15
     stores = []
@@ -267,7 +272,7 @@
                 values[n, at(k), :] = solved[n]
             return solved
 
-        value = lax.fori_loop(0, end - begin, up, value, unroll=5)
+        value = lax.fori_loop(0, end - begin, up, value, unroll=15)
         block = pl.ds(begin * lon_cells, (end - begin) * lon_cells)
         stores.append(pltpu.make_async_copy(
             values.at[:, block], out.at[:, block], store_sems.at[index]))

time: 25.6 us -> 21.9 us (0.86)
  Pallas kernels: 22.1 us -> 18.4 us
    pallas_call x1, Pallas kernels: 22.1 us -> 18.4 us  [shards(): pl.pallas_call(lambda *refs: step(tiles, *refs), out_shape=jax.ShapeDtype...]
where the time goes in v3:
time: 21.9 us; the launch traced here: 21.7 us
  Pallas kernels  18.4 us (84%)
  local copies, waits for them, and re-layouts  3.29 us (15%)
    pallas_call x1, Pallas kernels, shards(): pl.pallas_call(lambda *refs: step(tiles, *refs), out_shape=jax.ShapeDtype...  18.4 us
    unnamed x1, local copies, waits for them, and re-layouts  3.29 us

profile of v3, /device:TPU:0, one launch (start us, length us, event | category | flops | bytes accessed | tf_op | source)
XLA Modules:
  0.0 21.7 jit_solution(4354809813792761910)
XLA Ops:
  0.0 18.4 %ocean_step.1 = f32[4,1200,128]{2,1,0:T(8,128)} custom-call(f32[4,1200,128]{2,1,0:T(8,128)} %bitcast.26, f32[1200,128]{1,0:T(8,128)} %bitcast.27, f32[1200,128]{1,0:T(8,128)} %bitcast.28, f32[1200,128]{1,0:T(8,128)} %bitcast.29, f32[1200,128]{1,0:T(8,128)} %bitcast.30, f32[1200,128]{1,0:T(8,128)} %bitcast.31, s32[16,128]{1,0:T(8,128)} %refs_6_.1, ...), custom_call_target="tpu_custom_call" | custom-call | tf_op jit(solution)/shard_map/ocean_step/pallas_call | solution.py:305
  18.4 3.3 %copy.14 = f32[4,16,75,128]{3,1,2,0:T(8,128)} copy(f32[4,16,75,128]{3,1,2,0:T(8,128)} %bitcast.25) | data formatting | bytes 4915200

commit v4 on v3

--- a/solution.py
+++ b/solution.py
@@ -6,6 +6,7 @@
 from jax.sharding import PartitionSpec as P
 
 CAP = 64
+CHUNK = 15
 LANES = 128
 F32 = jnp.float32
 BF16 = jnp.bfloat16
@@ -87,10 +88,10 @@
 
 def step(tiles, *refs):
     sources, refs = refs[:12], refs[12:]
-    out, refs = refs[0], refs[1:]
+    values, gains, refs = refs[0], refs[1], refs[2:]
     held, refs = refs[:12], refs[12:]
-    (values, gains, factor, share, top, fold_out, fold_in, right_out, right_in, left_out, left_in,
-     send, received, load_sems, store_sems, out_sems, in_sems, pair_out, pair_in, own_sem) = refs
+    (factor, share, top, fold_out, fold_in, right_out, right_in, left_out, left_in,
+     send, received, load_sems, out_sems, in_sems, pair_out, pair_in, own_sem) = refs
     (tracer, east, north, kappa, mixing, thickness, depth_ref, air, tile, source, cells,
      weight) = held
     count, planes = tracer.shape[:2]
@@ -256,26 +257,31 @@
 
     value = lax.fori_loop(0, levels, down, (empty,) * count, unroll=15)
 
-    chunk = 15
+
+def finish(lon_cells, values, gains, out, solved, sems):
+    count, planes = values.shape[:2]
+    levels = planes // lon_cells
+
+    def at(k):
+        return pl.ds(pl.multiple_of(k * lon_cells, lon_cells), lon_cells)
+
     stores = []
-    value = (empty,) * count
-    for index, begin in enumerate(range(levels // chunk * chunk, -1, -chunk)):
-        end = min(begin + chunk, levels)
-        if begin == end:
-            continue
+    value = (jnp.zeros((lon_cells, LANES), F32),) * count
+    for index, end in enumerate(range(levels, 0, -CHUNK)):
+        begin = max(end - CHUNK, 0)
 
         def up(move, value, end=end):
             k = end - 1 - move
             gain = gains[at(k), :]
-            solved = tuple(values[n, at(k), :] + gain * value[n] for n in range(count))
+            value = tuple(values[n, at(k), :] + gain * value[n] for n in range(count))
             for n in range(count):
-                values[n, at(k), :] = solved[n]
-            return solved
-
-        value = lax.fori_loop(0, end - begin, up, value, unroll=15)
+                solved[n, at(k), :] = value[n]
+            return value
+
+        value = lax.fori_loop(0, end - begin, up, value, unroll=CHUNK)
         block = pl.ds(begin * lon_cells, (end - begin) * lon_cells)
         stores.append(pltpu.make_async_copy(
-            values.at[:, block], out.at[:, block], store_sems.at[index]))
+            solved.at[:, block], out.at[:, block], sems.at[index]))
         stores[-1].start()
     for store in stores:
         store.wait()
@@ -302,20 +308,28 @@
     fold = pltpu.VMEM((count + 3, lon_cells, LANES), F32)
     pairs = pltpu.VMEM((tiles, 8, LANES), F32)
     dma = pltpu.SemaphoreType.DMA
-    result = pl.pallas_call(
+    vmem = pl.BlockSpec(memory_space=pltpu.VMEM)
+    values, gains = pl.pallas_call(
         lambda *refs: step(tiles, *refs),
-        out_shape=jax.ShapeDtypeStruct(operands[0].shape, F32),
-        in_specs=[hbm] * 12, out_specs=hbm,
+        out_shape=(pltpu.VMEM(operands[0].shape, F32), flat),
+        in_specs=[hbm] * 12, out_specs=(vmem, vmem),
         scratch_shapes=[pltpu.VMEM(x.shape, x.dtype) for x in operands] + [
-            pltpu.VMEM(operands[0].shape, F32), flat, flat, flat, fold, fold, fold,
+            flat, flat, fold, fold, fold,
             pltpu.VMEM((count + 2, rows, LANES), F32), pltpu.VMEM((count + 2, rows, LANES), F32),
             pltpu.VMEM((count + 1, rows, LANES), F32), pltpu.VMEM((count + 1, rows, LANES), F32),
-            pairs, pairs, dma((12,)), dma((levels // 15 + 1,)), dma((3,)), dma((3,)),
+            pairs, pairs, dma((12,)), dma((3,)), dma((3,)),
             dma((tiles,)), dma((tiles,)), dma],
         compiler_params=pltpu.CompilerParams(
-            collective_id=0, has_side_effects=True, vmem_limit_bytes=60 << 20),
+            collective_id=0, has_side_effects=True, vmem_limit_bytes=32 << 20),
         name="ocean_step",
-    )(*operands)
+    )(*[pltpu.with_memory_space_constraint(x, pltpu.HBM) for x in operands])
+    result = pl.pallas_call(
+        lambda *refs: finish(lon_cells, *refs),
+        out_shape=pltpu.HBM(values.shape, F32),
+        in_specs=[vmem, vmem], out_specs=hbm,
+        scratch_shapes=[pltpu.VMEM(values.shape, F32), dma((pl.cdiv(levels, CHUNK),))],
+        name="finish",
+    )(*[pltpu.with_memory_space_constraint(x, pltpu.VMEM) for x in (values, gains)])
     return result.reshape(count, levels, lon_cells, LANES).transpose(0, 2, 1, 3)
 
 

time: 21.9 us -> 18.6 us (0.85)
  local copies, waits for them, and re-layouts: 3.29 us -> 0 us
    unnamed x1 -> x0, local copies, waits for them, and re-layouts: 3.29 us -> none
    pallas_call x1 -> x2, Pallas kernels: 18.4 us -> 18.4 us  [the longest x1 16.9 us: shards(): pl.pallas_call(lambda *refs: step(tiles, *refs), out_shape=(pltpu.VMEM(op...]
where the time goes in v4:
time: 18.6 us; the launch traced here: 18.4 us
  Pallas kernels  18.4 us (99%)
    pallas_call x1, Pallas kernels, shards(): pl.pallas_call(lambda *refs: step(tiles, *refs), out_shape=(pltpu.VMEM(op...  16.9 us
    pallas_call x1, Pallas kernels, shards(): pl.pallas_call(lambda *refs: finish(lon_cells, *refs), out_shape=pltpu.HB...  1.51 us

profile of v4, /device:TPU:0, one launch (start us, length us, event | category | flops | bytes accessed | tf_op | source)
XLA Modules:
  0.0 18.4 jit_solution(5443690349857800406)
XLA Ops:
  0.0 16.9 %ocean_step.1 = (f32[4,1200,128]{2,1,0:T(8,128)S(1)}, f32[1200,128]{1,0:T(8,128)S(1)}) custom-call(f32[4,1200,128]{2,1,0:T(8,128)} %bitcast.25, f32[1200,128]{1,0:T(8,128)} %bitcast.26, f32[1200,128]{1,0:T(8,128)} %bitcast.27, f32[1200,128]{1,0:T(8,128)} %bitcast.28, f32[1200,128]{1,0:T(8,128)} %bitcast.29, f32[1200,128]{1,0:T(8,128)} %bitcast.30, ...), custom_call_target="tpu_custom_call" | custom-call | tf_op jit(solution)/shard_map/ocean_step/pallas_call | solution.py:312
  16.9 1.5 %finish.1 = f32[4,1200,128]{2,1,0:T(8,128)} custom-call(f32[4,1200,128]{2,1,0:T(8,128)S(1)} %get-tuple-element.7.refs_0_, f32[1200,128]{1,0:T(8,128)S(1)} %get-tuple-element.8.refs_1_), custom_call_target="tpu_custom_call" | custom-call | tf_op jit(solution)/shard_map/finish/pallas_call | solution.py:326

commit v5 on v4

--- a/solution.py
+++ b/solution.py
@@ -101,7 +101,7 @@
 
     loads = [pltpu.make_async_copy(a, b, load_sems.at[i])
              for i, (a, b) in enumerate(zip(sources, held))]
-    for i in (7, 8, 9, 10, 11, 0, 2, 3, 1, 6, 5, 4):
+    for i in (7, 8, 9, 10, 11, 0, 3, 1, 6, 2, 5, 4):
         loads[i].start()
 
     me = lax.axis_index("lon")
@@ -119,7 +119,7 @@
         loads[i].wait()
     route(tiles, tile[...], source[...], cells[...], weight[...], air[...], send)
 
-    for i in (0, 2, 3, 1, 6):
+    for i in (0, 3, 1, 6):
         loads[i].wait()
     depth = depth_ref[...]
 
@@ -148,9 +148,6 @@
             device_id={"lon": device}, device_id_type=pl.DeviceIdType.MESH))
         copies[-1].start()
 
-    start(right_out, right_in, right)
-    start(left_out, left_in, left)
-
     @pl.loop(1, tiles)
     def _(hop):
         other = lax.rem(me + hop, tiles)
@@ -159,6 +156,11 @@
             recv_sem=pair_in.at[me], device_id={"lon": other},
             device_id_type=pl.DeviceIdType.MESH).start()
 
+    start(right_out, right_in, right)
+    start(left_out, left_in, left)
+
+
+    loads[2].wait()
     lane = iota((lon_cells, LANES), 1)
 
     def take(k, packed):

time: 18.6 us -> 18.4 us (0.989)
  Pallas kernels: 18.4 us -> 18.1 us
    pallas_call x1, Pallas kernels: 16.9 us -> 16.6 us  [shards(): pl.pallas_call(lambda *refs: step(tiles, *refs), out_shape=(pltpu.VMEM(op...]
where the time goes in v5:
time: 18.4 us; the launch traced here: 18.1 us
  Pallas kernels  18.1 us (98%)
    pallas_call x1, Pallas kernels, shards(): pl.pallas_call(lambda *refs: step(tiles, *refs), out_shape=(pltpu.VMEM(op...  16.6 us
    pallas_call x1, Pallas kernels, shards(): pl.pallas_call(lambda *refs: finish(lon_cells, *refs), out_shape=pltpu.HB...  1.51 us

profile of v5, /device:TPU:0, one launch (start us, length us, event | category | flops | bytes accessed | tf_op | source)
XLA Modules:
  0.0 18.1 jit_solution(3178687462986654371)
XLA Ops:
  0.0 16.6 %ocean_step.1 = (f32[4,1200,128]{2,1,0:T(8,128)S(1)}, f32[1200,128]{1,0:T(8,128)S(1)}) custom-call(f32[4,1200,128]{2,1,0:T(8,128)} %bitcast.25, f32[1200,128]{1,0:T(8,128)} %bitcast.26, f32[1200,128]{1,0:T(8,128)} %bitcast.27, f32[1200,128]{1,0:T(8,128)} %bitcast.28, f32[1200,128]{1,0:T(8,128)} %bitcast.29, f32[1200,128]{1,0:T(8,128)} %bitcast.30, ...), custom_call_target="tpu_custom_call" | custom-call | tf_op jit(solution)/shard_map/ocean_step/pallas_call | solution.py:314
  16.6 1.5 %finish.1 = f32[4,1200,128]{2,1,0:T(8,128)} custom-call(f32[4,1200,128]{2,1,0:T(8,128)S(1)} %get-tuple-element.7.refs_0_, f32[1200,128]{1,0:T(8,128)S(1)} %get-tuple-element.8.refs_1_), custom_call_target="tpu_custom_call" | custom-call | tf_op jit(solution)/shard_map/finish/pallas_call | solution.py:328
